TPU v7x, 128 devices: a whole 4x4x4 slice. The times are simulated.
128 devices in a mesh: dom: 16 (over z, y), sub: 4 (over x), rep: 2 (over core).
Axes of the slice: x: 4, y: 4, z: 4, core: 2. Of those that a mesh axis runs over, the one named last changes fastest.
Arguments:
- queries: bfloat16 [8192, 768], P(('dom', 'sub', 'rep')), may hold values from -5 to 5
- codebook: bfloat16 [192, 16, 4], replicated, may hold values from -1 to 1
- probes: int32 [8192, 8], P(('dom', 'sub', 'rep')), may hold values from 0 to 255, all different within a row; in each aligned block of 64 rows (0 to 63, 64 to 127, ...) at most 4 rows name the same one
- codes: int32 [256, 192, 2048], P(('dom', 'sub'), None, 'rep'), may hold values from 0 to 15
- part_sizes: int32 [256], P(('dom', 'sub')), may hold values from 1536 to 2048
Outputs:
- best_scores: float32 [8192, 100], P(('dom', 'sub', 'rep'))
Inputs may be any that keep to these rules, and one draw needn't show every extreme that they name: `probes`: each row names 8 different partitions. Among the rows of one device no partition is named more than 4 times, and in every draw some partition is named exactly 4 times by one device's rows.
All inputs are finite; a program needn't handle non-finite values.
Results may differ from a plain program's by a relative error of at most 0.00066.
Values may be sent and summed in bfloat16 or wider, within the bound.
A program may use at most 256 MiB of HBM per device.

v0:
```python
import jax
import jax.numpy as jnp
from jax import lax
from jax.sharding import PartitionSpec as P

TOPK = 100


MASKED = -1e30


def make_tables(vectors, codebook):
    n_rows = vectors.shape[0]
    n_groups = codebook.shape[0]
    pieces = vectors.reshape(n_rows, n_groups, codebook.shape[2])
    tables = jnp.einsum("rsj,scj->rsc", pieces, codebook, preferred_element_type=jnp.float32)
    return tables.reshape(n_rows, n_groups * codebook.shape[1]).astype(jnp.bfloat16)


def local(queries, codebook, probes, codes, part_sizes):
    n_dom = lax.axis_size("dom")
    n_sub = lax.axis_size("sub")
    n_rep = lax.axis_size("rep")
    n_dev = n_dom * n_sub
    own_rows = queries.shape[0]
    n_probe = probes.shape[1]
    part_dev, n_groups, half_slots = codes.shape
    n_cent = codebook.shape[1]
    n_parts = part_dev * n_dev
    capacity = max(2, 2 * own_rows * n_probe // n_parts)
    flat_parts = probes.reshape(-1)
    matches = (flat_parts[:, None] == jnp.arange(n_parts, dtype=jnp.int32)[None, :]).astype(
        jnp.int32
    )
    earlier = jnp.cumsum(matches, axis=0) - matches
    rank_index = jnp.sum(earlier * matches, axis=1)
    slot_index = flat_parts * capacity + rank_index
    source_rows = jnp.arange(own_rows * n_probe, dtype=jnp.int32) // n_probe
    relaid = lax.all_to_all(queries, "sub", split_axis=1, concat_axis=0, tiled=True)
    sub_groups = n_groups // n_sub
    own_book = lax.dynamic_slice_in_dim(codebook, lax.axis_index("sub") * sub_groups, sub_groups, 0)
    partial_tables = make_tables(relaid, own_book)
    tables = lax.all_to_all(partial_tables, "sub", split_axis=0, concat_axis=1, tiled=True)
    buffer = jnp.zeros((n_parts * capacity, tables.shape[1]), tables.dtype)
    arrived = lax.all_to_all(
        buffer.at[slot_index].set(tables[source_rows]),
        ("dom", "sub"),
        split_axis=0,
        concat_axis=0,
        tiled=True,
    )
    all_rows = lax.all_gather(arrived, "rep", axis=0, tiled=True)
    table_width = n_groups * n_cent
    grouped = all_rows.reshape(n_rep * n_dev, part_dev, capacity, table_width)
    slot_pos = lax.axis_index("rep") * half_slots + jnp.arange(half_slots, dtype=jnp.int32)
    centroid_ids = jnp.arange(n_cent, dtype=jnp.int32)
    pruned = []
    for which_part in range(part_dev):
        onehot = (codes[which_part][:, None, :] == centroid_ids[None, :, None]).astype(jnp.bfloat16)
        onehot = onehot.reshape(table_width, half_slots)
        row_block = grouped[:, which_part].reshape(n_rep * n_dev * capacity, table_width)
        scores = jnp.dot(row_block, onehot, preferred_element_type=jnp.float32)
        scores = jnp.where(slot_pos[None, :] < part_sizes[which_part], scores, MASKED)
        pruned.append(lax.top_k(scores, TOPK)[0])
    pruned = jnp.stack(pruned, axis=0).reshape(part_dev, n_rep, n_dev * capacity, TOPK)
    merged_halves = lax.all_to_all(pruned, "rep", split_axis=1, concat_axis=3, tiled=True)
    merged_halves = merged_halves.reshape(part_dev, n_dev * capacity, n_rep * TOPK)
    owner_best = lax.top_k(merged_halves, TOPK)[0]
    outgoing = owner_best.reshape(part_dev, n_dev, capacity, TOPK).transpose(1, 0, 2, 3)
    returned = lax.all_to_all(outgoing, ("dom", "sub"), split_axis=0, concat_axis=0, tiled=True)
    returned = returned.reshape(n_parts * capacity, TOPK)
    per_probe = returned[slot_index].reshape(own_rows, n_probe * TOPK)
    return lax.top_k(per_probe, TOPK)[0]


def solution(mesh):
    in_specs = (
        P(("dom", "sub", "rep"), None),
        P(),
        P(("dom", "sub", "rep"), None),
        P(("dom", "sub"), None, "rep"),
        P(("dom", "sub")),
    )
    out_specs = P(("dom", "sub", "rep"), None)
    return jax.shard_map(local, mesh=mesh, in_specs=in_specs, out_specs=out_specs, check_vma=False)
```

profile of v0, /device:TPU:0, one launch (start us, length us, event | category | flops | bytes accessed | tf_op | source)
XLA Modules:
  0.0 647.9 jit_solution(4181821170496120257)
XLA Ops:
  6.5 1.1 all_to_all.46
  7.6 0.7 copy.85
  8.3 4.4 all-to-all-start
  12.6 0.8 copy.80
  13.6 0.7 broadcast_multiply_fusion
  15.4 3.2 all-to-all-done
  19.6 1.2 copy.87
  20.8 3.5 all-to-all-start.1
  24.5 7.1 %all-to-all-done.1 = bf16[4,64,768]{2,1,0:T(8,128)(2,1)S(1)} async-done(((bf16[4,64,768]{2,1,0:T(8,128)(2,1)}), bf16[4,64,768]{2,1,0:T(8,128)(2,1)S(1)}, u32[]{:S(2)}, u32[]{:S(2)}) %all-to-all-start.1) | async-done | bytes 393248 | tf_op jit(solution)/shard_map/all_to_all | solution.py:43
  31.6 18.2 %scatter_custom_fusion = bf16[1024,3072]{1,0:T(8,128)(2,1)} fusion(s32[512]{0:T(512)S(1)} %bitcast.87, bf16[64,3072]{1,0:T(8,128)(2,1)S(1)} %bitcast.84, s32[1024]{0:T(1024)S(1)} %pad_clamp_fusion.1, bf16[]{:T(256)} %constant.77.clone.1), kind=kCustom, calls=%fused_computation.7 | custom fusion | bytes 6291458 | tf_op jit(solution)/shard_map/scatter | solution.py:46
  49.8 82.5 %all_to_all.64 = bf16[64,16,3072]{2,1,0:T(8,128)(2,1)} all-to-all(bf16[64,16,3072]{2,1,0:T(8,128)(2,1)} %bitcast.68), channel_id=1, replica_groups=mesh['dom'=16,'sub'=4,'rep'=2] {'dom','sub'}, dimensions={0} | all-to-all | bytes 12582912 | tf_op jit(solution)/shard_map/all_to_all | solution.py:45
  133.6 1.3 fusion.11
  134.8 1.2 fusion.9
  136.4 5.2 iota_compare_fusion.2
  141.6 5.0 iota_compare_fusion
  146.6 9.7 %all-gather.2.cloned.1.call-done = bf16[2048,3072]{1,0:T(8,128)(2,1)} async-done(((bf16[1024,3072]{1,0:T(8,128)(2,1)}), bf16[2048,3072]{1,0:T(8,128)(2,1)}) %all-gather.2.cloned.1.call-update) | async-done | bytes 12582928 | tf_op jit(solution)/shard_map/all_gather | solution.py:52
  156.3 21.1 %reshape.285 = bf16[128,4,4,3072]{3,2,1,0:T(4,128)(2,1)} reshape(bf16[2048,3072]{1,0:T(8,128)(2,1)} %all-gather.2.cloned.1.call-done) | data formatting | bytes 25165824 | tf_op jit(solution)/shard_map/reshape | solution.py:54
  177.4 11.1 %fusion.13 = (bf16[128,1,4,3072]{3,2,1,0:T(4,128)(2,1)S(1)}, bf16[128,1,4,3072]{3,2,1,0:T(4,128)(2,1)}, bf16[128,1,4,3072]{3,2,1,0:T(4,128)(2,1)}, bf16[128,1,4,3072]{3,2,1,0:T(4,128)(2,1)}) fusion(bf16[128,4,4,3072]{3,2,1,0:T(4,128)(2,1)} %reshape.285), kind=kLoop, calls=%fused_computation.46 | loop fusion | bytes 25165824 | tf_op jit(solution)/shard_map/slice | solution.py:61
  188.5 2.4 reshape_squeeze.12
  190.9 6.3 convolution_select_fusion.3
  197.2 1.9 copy.97
  199.3 74.9 %top_k.46 = (f32[512,1024]{0,1:T(8,128)}, s32[512,1024]{0,1:T(8,128)}) sort(f32[512,1024]{0,1:T(8,128)} %copy.97, s32[512,1024]{0,1:T(8,128)S(1)} %iota.90.clone), dimensions={1}, to_apply=%region_4.5 | sort | flops 9961472 | bytes 8388608 | tf_op jit(solution)/shard_map/top_k | solution.py:64
  274.2 2.9 copy.99
  277.1 1.0 top_k.62
  278.2 5.9 reshape_squeeze.13
  284.1 7.6 %convolution_select_fusion.2 = f32[512,1024]{1,0:T(8,128)} fusion(bf16[512,3072]{1,0:T(8,128)(2,1)} %reshape_squeeze.13, pred[3072,1024]{1,0:T(8,128)(4,1)} %bitcast.73, pred[1024]{0:T(1024)(128)(4,1)S(1)} %get-tuple-element.51), kind=kOutput, calls=%fused_computation.12 | convolution fusion | flops 3221749760 | bytes 8389632 | tf_op jit(solution)/shard_map/dot_general | solution.py:62
  291.7 3.0 copy.102
  294.7 75.0 %top_k.48 = (f32[512,1024]{0,1:T(8,128)}, s32[512,1024]{0,1:T(8,128)}) sort(f32[512,1024]{0,1:T(8,128)} %copy.102, s32[512,1024]{0,1:T(8,128)S(1)} %iota.90.clone), dimensions={1}, to_apply=%region_5.6 | sort | flops 9961472 | bytes 8388608 | tf_op jit(solution)/shard_map/top_k | solution.py:64
  369.7 2.9 copy.104
  372.6 1.0 top_k.63
  373.7 6.0 reshape_squeeze.14
  379.7 7.7 %convolution_select_fusion.1 = f32[512,1024]{1,0:T(8,128)} fusion(bf16[512,3072]{1,0:T(8,128)(2,1)} %reshape_squeeze.14, pred[3072,1024]{1,0:T(8,128)(4,1)} %bitcast.72, pred[1024]{0:T(1024)(128)(4,1)S(1)} %get-tuple-element.50), kind=kOutput, calls=%fused_computation.11 | convolution fusion | flops 3221749760 | bytes 8389632 | tf_op jit(solution)/shard_map/dot_general | solution.py:62
  387.4 2.9 copy.107
  390.3 75.2 %top_k.50 = (f32[512,1024]{0,1:T(8,128)}, s32[512,1024]{0,1:T(8,128)}) sort(f32[512,1024]{0,1:T(8,128)} %copy.107, s32[512,1024]{0,1:T(8,128)S(1)} %iota.90.clone), dimensions={1}, to_apply=%region_6.7 | sort | flops 9961472 | bytes 8388608 | tf_op jit(solution)/shard_map/top_k | solution.py:64
  465.5 2.9 copy.109
  468.4 1.0 top_k.68
  469.6 5.9 reshape_squeeze.15
  475.5 7.7 %convolution_select_fusion = f32[512,1024]{1,0:T(8,128)} fusion(bf16[512,3072]{1,0:T(8,128)(2,1)} %reshape_squeeze.15, pred[3072,1024]{1,0:T(8,128)(4,1)} %bitcast.71, pred[1024]{0:T(1024)(128)(4,1)S(1)} %get-tuple-element.49), kind=kOutput, calls=%fused_computation.10 | convolution fusion | flops 3221749760 | bytes 8389632 | tf_op jit(solution)/shard_map/dot_general | solution.py:62
  483.2 2.9 copy.112
  486.1 74.9 %top_k.56 = (f32[512,1024]{0,1:T(8,128)}, s32[512,1024]{0,1:T(8,128)}) sort(f32[512,1024]{0,1:T(8,128)} %copy.112, s32[512,1024]{0,1:T(8,128)S(1)} %iota.90.clone), dimensions={1}, to_apply=%region_7.8 | sort | flops 9961472 | bytes 8388608 | tf_op jit(solution)/shard_map/top_k | solution.py:64
  561.0 1.9 copy.114
  563.9 4.4 all_to_all.65
  568.5 24.1 %top_k.58 = (f32[4,256,200]{1,2,0:T(8,128)S(1)}, s32[4,256,200]{1,2,0:T(8,128)}) sort(f32[4,256,200]{1,2,0:T(8,128)S(1)} %copy.119, s32[4,256,200]{1,2,0:T(8,128)S(1)} %iota.94.clone), dimensions={2}, to_apply=%region_8.9 | sort | flops 3686400 | bytes 3276800 | tf_op jit(solution)/shard_map/top_k | solution.py:68
  592.9 0.9 copy.96
  593.8 10.4 %all-to-all-start.4 = ((f32[64,4,4,100]{3,2,1,0:T(4,128)}), f32[64,4,4,100]{3,2,1,0:T(4,128)S(1)}, u32[]{:S(2)}, u32[]{:S(2)}) async-start(f32[64,4,4,100]{3,2,1,0:T(4,128)} %copy.96), calls=%async_computation.4 | async-start | bytes 1048576 | tf_op jit(solution)/shard_map/all_to_all | solution.py:70
  604.2 13.6 %all-to-all-done.4 = f32[64,4,4,100]{3,2,1,0:T(4,128)S(1)} async-done(((f32[64,4,4,100]{3,2,1,0:T(4,128)}), f32[64,4,4,100]{3,2,1,0:T(4,128)S(1)}, u32[]{:S(2)}, u32[]{:S(2)}) %all-to-all-start.4) | async-done | bytes 409632 | tf_op jit(solution)/shard_map/all_to_all | solution.py:70
  617.9 1.2 gather_fusion
  619.3 20.9 %top_k.60 = (f32[64,800]{1,0:T(8,128)S(1)}, s32[64,800]{1,0:T(8,128)}) sort(f32[64,800]{1,0:T(8,128)S(1)} %reshape.289, s32[64,800]{1,0:T(8,128)S(1)} %iota.95), dimensions={1}, to_apply=%region_9.10 | sort | flops 819200 | bytes 819200 | tf_op jit(solution)/shard_map/top_k | solution.py:73
  (51 shorter events, 7.0 us)
Async XLA Ops:
  6.5 7.7 %copy-start = (bf16[192,16,4]{0,2,1:T(4,128)(2,1)S(1)}, bf16[192,16,4]{0,2,1:T(4,128)(2,1)}, u32[]{:S(2)}) copy-start(bf16[192,16,4]{0,2,1:T(4,128)(2,1)} %param.6) | copy-start | bytes 73732
  8.3 10.4 %all-to-all-start = ((bf16[64,4,192]{2,0,1:T(8,128)(2,1)}), bf16[64,4,192]{2,0,1:T(8,128)(2,1)S(1)}, u32[]{:S(2)}, u32[]{:S(2)}) async-start(bf16[64,4,192]{2,0,1:T(8,128)(2,1)} %copy.85), calls=%async_computation | async-start | bytes 262144 | tf_op jit(solution)/shard_map/all_to_all | solution.py:39
  20.8 10.8 %all-to-all-start.1 = ((bf16[4,64,768]{2,1,0:T(8,128)(2,1)}), bf16[4,64,768]{2,1,0:T(8,128)(2,1)S(1)}, u32[]{:S(2)}, u32[]{:S(2)}) async-start(bf16[4,64,768]{2,1,0:T(8,128)(2,1)} %copy.87), calls=%async_computation.1 | async-start | bytes 786432 | tf_op jit(solution)/shard_map/all_to_all | solution.py:43
  24.2 132.0 %all-gather.2.cloned.1.call-start = ((), (), s32[]{:S(2)}) async-start(), calls=%async_computation.5 | async-start | bytes 18874368 | tf_op jit(solution)/shard_map/all_gather | solution.py:52
  132.3 0.7 copy-start.3
  132.3 3.7 copy-start.2
  592.5 48.3 %copy-start.1 = (bf16[192,16,4]{0,2,1:T(4,128)(2,1)S(1)}, bf16[192,16,4]{0,2,1:T(4,128)(2,1)}, u32[]{:S(2)}) copy-start(bf16[192,16,4]{0,2,1:T(4,128)(2,1)} %param.6) | copy-start | bytes 73732
  593.8 24.1 %all-to-all-start.4 = ((f32[64,4,4,100]{3,2,1,0:T(4,128)}), f32[64,4,4,100]{3,2,1,0:T(4,128)S(1)}, u32[]{:S(2)}, u32[]{:S(2)}) async-start(f32[64,4,4,100]{3,2,1,0:T(4,128)} %copy.96), calls=%async_computation.4 | async-start | bytes 1048576 | tf_op jit(solution)/shard_map/all_to_all | solution.py:70
Sparse Core Ops, SparseCore 0:
  132.4 23.7 all-gather.1
where the time goes:
time: 653 us; the launch traced here: 648 us
  other arithmetic  359 us (55%)
  local copies, waits for them, and re-layouts  106 us (16%)
  blocking collectives  86.9 us (13%)
  waiting for transfers between devices  33.6 us (5%)
  matrix products  29.6 us (5%)
  starting transfers between devices  18.5 us (3%)
  between operations  13.9 us (2%)
    top_k x4, other arithmetic, local(): pruned.append(lax.top_k(scores, TOPK)[0])  300 us
    all_to_all x1, blocking collectives, local(): lax.all_to_all(buffer.at[slot_index].set(tables[source_rows]), ('dom', 's...  82.5 us
    dot_general x4, matrix products, local(): scores = jnp.dot(row_block, onehot, preferred_element_type=jnp.float32)  29.3 us
    top_k x1, other arithmetic, local(): owner_best = lax.top_k(merged_halves, TOPK)[0]  24.1 us
    reshape x1, local copies, waits for them, and re-layouts, local(): grouped = all_rows.reshape(n_rep * n_dev, part_dev, capacity, table_width)  21.1 us
    top_k x1, other arithmetic, local(): return lax.top_k(per_probe, TOPK)[0]  20.9 us
    another operation x4, local copies, waits for them, and re-layouts, local(): grouped[:, which_part].reshape(n_rep * n_dev * capacity, table_width)  20.2 us
    scatter x1, local copies, waits for them, and re-layouts, local(): buffer.at[slot_index].set(tables[source_rows])  18.2 us
  transfers between devices with their start and end apart: 4, of which 4 were waited for; matrix products, arithmetic and copies ran while one was open for 3% of the time, Pallas kernels for 0%

commit v1 on v0

v1 whole, which is shorter than its diff:
```python
import functools

import jax
import jax.numpy as jnp
from jax import lax
from jax.experimental import pallas as pl
from jax.experimental.pallas import tpu as pltpu
from jax.sharding import PartitionSpec as P

TOPK = 100
MASKED = -1e30
RANKS = 128
LANES = 128
SUBL = 8


def batcher(n):
    pairs = []

    def merge(lo, cnt, r):
        step = r * 2
        if step < cnt:
            merge(lo, cnt, step)
            merge(lo + r, cnt, step)
            for i in range(lo + r, lo + cnt - r, step):
                pairs.append((i, i + r))
        else:
            pairs.append((lo, lo + r))

    def sort(lo, cnt):
        if cnt > 1:
            m = cnt // 2
            sort(lo, m)
            sort(lo + m, m)
            merge(lo, cnt, 1)

    sort(0, n)
    return pairs


SORT32 = batcher(32)


def exchange(x, pairs):
    for i, j in pairs:
        a, b = x[i], x[j]
        x[i] = jnp.maximum(a, b)
        x[j] = jnp.minimum(a, b)
    return x


def clean(x):
    d = len(x) // 2
    while d:
        exchange(x, [(i, i + d) for i in range(len(x)) if not i & d])
        d //= 2
    return x


def prep_kernel(n_cap, q_ref, probes_ref, send_ref, idx_ref):
    rows, width = q_ref.shape
    slots = send_ref.shape[0]
    n = lax.broadcasted_iota(jnp.int32, (rows, slots), 1)
    part = n // n_cap
    rank_of = (n % n_cap).astype(jnp.float32)
    probes = probes_ref[...]
    named = part == probes[:, 0:1]
    for k in range(1, probes.shape[1]):
        named = named | (part == probes[:, k : k + 1])
    before = (
        lax.broadcasted_iota(jnp.int32, (rows, rows), 0) > lax.broadcasted_iota(jnp.int32, (rows, rows), 1)
    ).astype(jnp.float32).astype(jnp.bfloat16)
    rank = jnp.dot(before, named.astype(jnp.float32).astype(jnp.bfloat16), preferred_element_type=jnp.float32)
    chosen = jnp.where(named & (rank == rank_of), 1.0, 0.0)
    nf = n.astype(jnp.float32)
    for k in range(probes.shape[1]):
        hit = jnp.where(part == probes[:, k : k + 1], chosen, 0.0)
        idx_ref[:, k : k + 1] = jnp.sum(hit * nf, axis=1, keepdims=True).astype(jnp.int32)
    a = lax.broadcasted_iota(jnp.int32, (width, width), 0)
    b = lax.broadcasted_iota(jnp.int32, (width, width), 1)
    groups = width // 4
    j = (b >= groups).astype(jnp.int32) + (b >= 2 * groups).astype(jnp.int32) + (b >= 3 * groups).astype(jnp.int32)
    perm = jnp.where(a == (b - groups * j) * 4 + j, 1.0, 0.0).astype(jnp.bfloat16)
    moved = jnp.dot(q_ref[...], perm, preferred_element_type=jnp.float32).astype(jnp.bfloat16)
    picked = lax.dot_general(
        chosen.astype(jnp.bfloat16), moved, (((0,), (0,)), ((), ())), preferred_element_type=jnp.float32
    )
    send_ref[...] = picked.astype(jnp.bfloat16)


def prep(queries, probes, n_slots, n_cap):
    return pl.pallas_call(
        functools.partial(prep_kernel, n_cap),
        out_shape=(
            jax.ShapeDtypeStruct((n_slots, queries.shape[1]), jnp.bfloat16),
            jax.ShapeDtypeStruct(probes.shape, jnp.int32),
        ),
        in_specs=[pl.BlockSpec(memory_space=pltpu.VMEM)] * 2,
        out_specs=[pl.BlockSpec(memory_space=pltpu.VMEM)] * 2,
        compiler_params=pltpu.CompilerParams(vmem_limit_bytes=40 << 20),
        name="prep",
    )(queries, probes)


def sort_block(s_ref, x_ref, b, h):
    groups = s_ref.shape[1] // 32

    @pl.loop(0, groups)
    def _(g):
        x = exchange([s_ref[b, g * 32 + i] for i in range(32)], SORT32)
        for i in range(32):
            s_ref[b, g * 32 + i] = x[i]

    @pl.loop(0, groups // 2)
    def _(g):
        base = g * 64
        low = []
        high = []
        for i in range(32):
            u, v = s_ref[b, base + i], s_ref[b, base + 63 - i]
            high.append(jnp.maximum(u, v))
            low.append(jnp.minimum(u, v))
        clean(high)
        clean(low)
        for i in range(32):
            s_ref[b, base + i] = high[i]
            s_ref[b, base + 32 + i] = low[i]

    @pl.loop(0, groups // 4)
    def _(g):
        base = g * 128

        @pl.loop(0, 32, unroll=8)
        def _(i):
            u0, u1 = s_ref[b, base + i], s_ref[b, base + 32 + i]
            v0, v1 = s_ref[b, base + 127 - i], s_ref[b, base + 95 - i]
            h0, h1 = jnp.maximum(u0, v0), jnp.maximum(u1, v1)
            l0, l1 = jnp.minimum(u0, v0), jnp.minimum(u1, v1)
            x_ref[h, i] = jnp.maximum(h0, h1)
            x_ref[h, 32 + i] = jnp.minimum(h0, h1)
            x_ref[h, 64 + i] = jnp.maximum(l0, l1)
            x_ref[h, 96 + i] = jnp.minimum(l0, l1)

        @pl.loop(0, 4)
        def _(k):
            x = clean([x_ref[h, k * 32 + i] for i in range(32)])
            for i in range(32):
                s_ref[b, base + k * 32 + i] = x[i]

    @pl.loop(0, 32, unroll=8)
    def _(i):
        t = [jnp.maximum(s_ref[b, i + 32 * k], s_ref[b, 255 - i - 32 * k]) for k in range(4)]
        clean(t)
        for k in range(4):
            x_ref[h, i + 32 * k] = t[k]

    @pl.loop(0, 4)
    def _(k):
        x = clean([x_ref[h, k * 32 + i] for i in range(32)])
        for i in range(32):
            x_ref[h, k * 32 + i] = x[i]


def merge_pair(x_ref, b0, b1, level):
    bit = 1 << level
    lower = (lax.broadcasted_iota(jnp.int32, (SUBL, LANES), 0) & bit) == 0

    def joined(i, m):
        first = jnp.where(lower, x_ref[b0, i], x_ref[b1, i])
        second = jnp.where(lower, pltpu.roll(x_ref[b0, m], SUBL - bit, 0), pltpu.roll(x_ref[b1, m], bit, 0))
        return jnp.maximum(first, second)

    @pl.loop(0, 64, unroll=4)
    def _(i):
        m = 127 - i
        s, t = joined(i, m), joined(m, i)
        x_ref[b0, i] = s
        x_ref[b0, m] = t

    @pl.loop(0, 32, unroll=8)
    def _(i):
        t = clean([x_ref[b0, i + 32 * k] for k in range(4)])
        for k in range(4):
            x_ref[b0, i + 32 * k] = t[k]

    @pl.loop(0, 4)
    def _(k):
        x = clean([x_ref[b0, k * 32 + i] for i in range(32)])
        for i in range(32):
            x_ref[b0, k * 32 + i] = x[i]


def score_kernel(n_cap, sizes_ref, table_ref, q_ref, own_ref, peer_ref, out_ref, d_ref, s_ref, x_ref, z_ref):
    p = pl.program_id(0)
    groups, half = own_ref.shape[1:]
    part_dev = pl.num_programs(0)
    tiles = half // LANES

    @pl.loop(0, groups // 16)
    def _(g):
        rows = pl.ds(pl.multiple_of(g * 16, 16), 16)
        tab = [table_ref[j, rows, :] for j in range(4)]
        for t in range(2 * tiles):
            ref = own_ref if t < tiles else peer_ref
            c = ref[0, rows, (t % tiles) * LANES : (t % tiles + 1) * LANES]
            for j in range(4):
                val = jnp.take_along_axis(tab[j], c, axis=1)
                d_ref[pl.ds(pl.multiple_of(j * groups + g * 16, 16), 16), t * LANES : (t + 1) * LANES] = val.astype(
                    jnp.bfloat16
                )

    all_rows = q_ref.shape[0]
    m = lax.broadcasted_iota(jnp.int32, (256, all_rows), 0)
    src = (m // 128) * 32 + m % 32
    want = src * (part_dev * n_cap) + p * n_cap + (m % 128) // 32
    pick = jnp.where(lax.broadcasted_iota(jnp.int32, (256, all_rows), 1) == want, 1.0, 0.0).astype(jnp.bfloat16)
    mine = jnp.dot(pick, q_ref[...], preferred_element_type=jnp.float32).astype(jnp.bfloat16)

    @pl.loop(0, 2 * half // 256)
    def _(t):
        cols = pl.ds(pl.multiple_of(t * 256, 256), 256)
        sc = jnp.dot(mine, d_ref[:, cols], preferred_element_type=jnp.float32)
        sc = sc.T
        per_half = half // 256
        which = t // per_half
        slot = lax.broadcasted_iota(jnp.int32, (256, LANES), 0) + (t - which * per_half) * 256
        ok = slot < sizes_ref[which, p]
        for h in range(2):
            blk = jnp.where(ok, sc[:, h * LANES : (h + 1) * LANES], MASKED)
            s_ref[h, pl.ds(t * 32, 32)] = blk.reshape(32, SUBL, LANES)

    for h in range(2):
        sort_block(s_ref, x_ref, h, p * 2 + h)

    @pl.when(p == part_dev - 1)
    def _():
        for b in range(0, 8, 2):
            merge_pair(x_ref, b, b + 1, 2)
        for b in range(0, 8, 4):
            merge_pair(x_ref, b, b + 2, 1)
        merge_pair(x_ref, 0, 4, 0)
        z_ref[...] = x_ref[0].reshape(RANKS * SUBL, LANES)
        for blk in range(8):
            u = 4 * (blk & 1) + (blk & 2) + (blk >> 2)
            got = z_ref[pl.ds(u, RANKS, stride=SUBL), :].T
            for r in range(n_cap):
                base = (blk & 1) * 32 * 16 + (blk >> 1) * n_cap + r
                out_ref[pl.ds(base, 32, stride=16), :] = got[r * 32 : (r + 1) * 32, :]


def score(sizes, table, rows, own, peer, n_cap):
    part_dev, groups, half = own.shape
    n_rows, width = rows.shape
    blk = pl.BlockSpec((1, groups, half), lambda p: (p, 0, 0))
    return pl.pallas_call(
        functools.partial(score_kernel, n_cap),
        grid=(part_dev,),
        out_shape=jax.ShapeDtypeStruct((n_rows, RANKS), jnp.float32),
        in_specs=[
            pl.BlockSpec(memory_space=pltpu.SMEM),
            pl.BlockSpec(memory_space=pltpu.VMEM),
            pl.BlockSpec(memory_space=pltpu.VMEM),
            blk,
            blk,
        ],
        out_specs=pl.BlockSpec(memory_space=pltpu.VMEM),
        scratch_shapes=[
            pltpu.VMEM((width, 2 * half), jnp.bfloat16),
            pltpu.VMEM((2, 2 * half // SUBL, SUBL, LANES), jnp.float32),
            pltpu.VMEM((8, RANKS, SUBL, LANES), jnp.float32),
            pltpu.VMEM((RANKS * SUBL, LANES), jnp.float32),
        ],
        compiler_params=pltpu.CompilerParams(vmem_limit_bytes=48 << 20),
        name="score",
    )(sizes, table, rows, own, peer)


def merge_kernel(idx_ref, r_ref, out_ref, l_ref):
    rows = out_ref.shape[0]
    total = l_ref.shape[0]

    @pl.loop(0, total, unroll=8)
    def _(i):
        l_ref[pl.ds(i, 1), :] = r_ref[pl.ds(idx_ref[i], 1), :]

    lists = l_ref[...]
    while lists.shape[0] > rows:
        h = lists.shape[0] // 2
        lane = lax.broadcasted_iota(jnp.int32, (h, RANKS), 1)
        a, b = lists[:h], lists[h:]
        lists = jnp.maximum(a, jnp.take_along_axis(b, RANKS - 1 - lane, axis=1))
        d = RANKS // 2
        while d:
            other = jnp.take_along_axis(lists, lane ^ d, axis=1)
            lists = jnp.where((lane & d) == 0, jnp.maximum(lists, other), jnp.minimum(lists, other))
            d //= 2
    out_ref[...] = lists[:, : out_ref.shape[1]]


def merge(idx, returned, n_rows):
    total = idx.shape[0]
    return pl.pallas_call(
        merge_kernel,
        out_shape=jax.ShapeDtypeStruct((n_rows, TOPK), jnp.float32),
        in_specs=[pl.BlockSpec(memory_space=pltpu.SMEM), pl.BlockSpec(memory_space=pltpu.VMEM)],
        out_specs=pl.BlockSpec(memory_space=pltpu.VMEM),
        scratch_shapes=[pltpu.VMEM((total, RANKS), jnp.float32)],
        name="merge",
    )(idx, returned)


def local(queries, codebook, probes, codes, part_sizes):
    n_dev = lax.axis_size("dom") * lax.axis_size("sub")
    rep = lax.axis_index("rep")
    own_rows, width = queries.shape
    n_probe = probes.shape[1]
    part_dev, n_groups, half = codes.shape
    n_cent = codebook.shape[1]
    n_parts = part_dev * n_dev
    n_cap = max(2, 2 * own_rows * n_probe // n_parts)
    peer = lax.ppermute(codes, "rep", [(0, 1), (1, 0)])
    send, idx = prep(queries, probes, n_parts * n_cap, n_cap)
    arrived = lax.all_to_all(
        send.reshape(n_dev, part_dev * n_cap, width), ("dom", "sub"), split_axis=0, concat_axis=0, tiled=True
    ).reshape(n_parts * n_cap, width)
    table = jnp.pad(codebook.astype(jnp.float32).transpose(2, 0, 1), ((0, 0), (0, 0), (0, LANES - n_cent)))
    sizes = jnp.stack([part_sizes - rep * half, part_sizes - (1 - rep) * half])
    best = score(sizes, table, arrived, codes, peer, n_cap)
    returned = lax.all_to_all(
        best.reshape(n_dev, part_dev * n_cap, RANKS), ("dom", "sub"), split_axis=0, concat_axis=0, tiled=True
    ).reshape(n_parts * n_cap, RANKS)
    return merge(idx.T.reshape(-1), returned, own_rows)


def solution(mesh):
    in_specs = (
        P(("dom", "sub", "rep"), None),
        P(),
        P(("dom", "sub", "rep"), None),
        P(("dom", "sub"), None, "rep"),
        P(("dom", "sub")),
    )
    out_specs = P(("dom", "sub", "rep"), None)
    return jax.shard_map(local, mesh=mesh, in_specs=in_specs, out_specs=out_specs, check_vma=False)
```

time: 653 us -> 109 us (0.17)
  other arithmetic: 359 us -> 0.05 us
  local copies, waits for them, and re-layouts: 106 us -> 5.28 us
  blocking collectives: 86.9 us -> 0 us
  Pallas kernels: 0 us -> 48.5 us
  matrix products: 29.6 us -> 0 us
  between operations: 13.9 us -> 0.08 us
    top_k x6 -> x0, other arithmetic: 345 us -> none  [the longest x4 300 us: local(): pruned.append(lax.top_k(scores, TOPK)[0])]
    all_to_all x2 -> x0, blocking collectives: 86.9 us -> none  [the longest x1 82.5 us: local(): lax.all_to_all(buffer.at[slot_index].set(tables[source_rows]), ('dom', 's...]
    pallas_call x0 -> x3, Pallas kernels: none -> 48.5 us  [the longest x1 41.8 us: score(): pl.pallas_call(functools.partial(score_kernel, n_cap), grid=(part_dev,),...]
    dot_general x5 -> x0, matrix products: 29.6 us -> none  [the longest x4 29.3 us: local(): scores = jnp.dot(row_block, onehot, preferred_element_type=jnp.float32)]
    another operation x15 -> x0, local copies, waits for them, and re-layouts: 21.4 us -> none  [the longest x4 20.2 us: local(): grouped[:, which_part].reshape(n_rep * n_dev * capacity, table_width)]
    reshape x3 -> x1, local copies, waits for them, and re-layouts: 21.4 us -> 0.66 us  [local(): return merge(idx.T.reshape(-1), returned, own_rows)]
    scatter x1 -> x0, local copies, waits for them, and re-layouts: 18.2 us -> none  [local(): buffer.at[slot_index].set(tables[source_rows])]
    top_k x11 -> x0, local copies, waits for them, and re-layouts: 14.6 us -> none  [the longest x8 13.6 us: local(): pruned.append(lax.top_k(scores, TOPK)[0])]
  transfers between devices with their start and end apart: 4 -> 3, of which waited for: 4 -> 2; matrix products, arithmetic and copies ran while one was open for 3% -> 2% of each run, Pallas kernels for 0% -> 2%
where the time goes in v1:
time: 109 us; the launch traced here: 108 us
  Pallas kernels  48.5 us (44%)
  waiting for transfers between devices  37.3 us (34%)
  starting transfers between devices  16.8 us (15%)
  local copies, waits for them, and re-layouts  5.28 us (5%)
    pallas_call x1, Pallas kernels, score(): pl.pallas_call(functools.partial(score_kernel, n_cap), grid=(part_dev,),...  41.8 us
    all_to_all x1, waiting for transfers between devices, local(): lax.all_to_all(send.reshape(n_dev, part_dev * n_cap, width), ('dom', 'sub...  24.8 us
    all_to_all x1, waiting for transfers between devices, local(): lax.all_to_all(best.reshape(n_dev, part_dev * n_cap, RANKS), ('dom', 'sub...  12.5 us
    all_to_all x1, starting transfers between devices, local(): lax.all_to_all(send.reshape(n_dev, part_dev * n_cap, width), ('dom', 'sub...  11.5 us
    all_to_all x1, starting transfers between devices, local(): lax.all_to_all(best.reshape(n_dev, part_dev * n_cap, RANKS), ('dom', 'sub...  5.33 us
    unnamed x12, local copies, waits for them, and re-layouts  4.55 us
    pallas_call x1, Pallas kernels, merge(): pl.pallas_call(merge_kernel, out_shape=jax.ShapeDtypeStruct((n_rows, TOPK...  4.03 us
    pallas_call x1, Pallas kernels, prep(): pl.pallas_call(functools.partial(prep_kernel, n_cap), out_shape=(jax.Shap...  2.65 us
  transfers between devices with their start and end apart: 3, of which 2 were waited for; matrix products, arithmetic and copies ran while one was open for 2% of the time, Pallas kernels for 2%

profile of v1, /device:TPU:0, one launch (start us, length us, event | category | flops | bytes accessed | tf_op | source)
XLA Modules:
  0.0 108.1 jit_solution(4768797952757986764)
XLA Ops:
  0.0 0.0 copy-start.3
  0.0 0.0 copy-start.4
  0.0 0.0 collective-permute-start
  0.0 0.8 copy.8.probes_ref
  0.8 0.0 copy-start.1
  0.8 0.9 copy-done.1
  1.7 2.6 %prep.1 = (bf16[1024,768]{1,0:T(8,128)(2,1)}, s32[64,8]{1,0:T(8,128)S(1)}) custom-call(bf16[64,768]{1,0:T(8,128)(2,1)S(1)} %copy-done.1, s32[64,8]{1,0:T(8,128)S(1)} %copy.8.probes_ref), custom_call_target="tpu_custom_call" | custom-call | tf_op jit(solution)/shard_map/prep/pallas_call | solution.py:92
  4.3 11.5 %all-to-all-start = ((bf16[64,16,768]{2,1,0:T(8,128)(2,1)}), bf16[64,16,768]{2,1,0:T(8,128)(2,1)S(1)}, u32[]{:S(2)}, u32[]{:S(2)}) async-start(bf16[64,16,768]{2,1,0:T(8,128)(2,1)} %bitcast.4), calls=%async_computation | async-start | bytes 3145728 | tf_op jit(solution)/shard_map/all_to_all | solution.py:323
  15.9 0.0 copy-done.3
  15.9 0.2 copy.10
  16.1 0.0 copy-done.4
  16.1 24.8 %all-to-all-done = bf16[64,16,768]{2,1,0:T(8,128)(2,1)S(1)} async-done(((bf16[64,16,768]{2,1,0:T(8,128)(2,1)}), bf16[64,16,768]{2,1,0:T(8,128)(2,1)S(1)}, u32[]{:S(2)}, u32[]{:S(2)}) %all-to-all-start) | async-done | bytes 1572896 | tf_op jit(solution)/shard_map/all_to_all | solution.py:323
  40.9 0.0 collective-permute-done.peer_ref
  40.9 0.0 copy-start
  40.9 1.9 %copy-done = s32[4,192,1024]{2,1,0:T(8,128)S(1)} copy-done((s32[4,192,1024]{2,1,0:T(8,128)S(1)}, s32[4,192,1024]{2,1,0:T(8,128)}, u32[]{:S(2)}) %copy-start) | copy-done | bytes 3145752
  42.8 41.8 %score.1 = f32[1024,128]{1,0:T(8,128)} custom-call(s32[2,4]{1,0:T(2,128)S(1)} %pad_add_fusion.sizes_ref, f32[4,192,128]{2,1,0:T(8,128)S(1)} %pad_convert_fusion.table_ref, bf16[1024,768]{1,0:T(8,128)(2,1)S(1)} %bitcast.10, s32[4,192,1024]{2,1,0:T(8,128)S(1)} %copy-done, s32[4,192,1024]{2,1,0:T(8,128)} %collective-permute-done.peer_ref), custom_call_target="tpu_custom_call" | custom-call | tf_op jit(solution)/shard_map/score/pallas_call | solution.py:255
  84.7 5.3 %all-to-all-start.1 = ((f32[64,16,128]{2,1,0:T(8,128)}), f32[64,16,128]{2,1,0:T(8,128)S(1)}, u32[]{:S(2)}, u32[]{:S(2)}) async-start(f32[64,16,128]{2,1,0:T(8,128)} %bitcast.6), calls=%async_computation.1 | async-start | bytes 1048576 | tf_op jit(solution)/shard_map/all_to_all | solution.py:329
  90.0 0.1 copy.9
  90.1 0.7 reshape.15.idx_ref
  90.7 12.5 %all-to-all-done.1 = f32[64,16,128]{2,1,0:T(8,128)S(1)} async-done(((f32[64,16,128]{2,1,0:T(8,128)}), f32[64,16,128]{2,1,0:T(8,128)S(1)}, u32[]{:S(2)}, u32[]{:S(2)}) %all-to-all-start.1) | async-done | bytes 524320 | tf_op jit(solution)/shard_map/all_to_all | solution.py:329
  103.2 0.0 copy-start.2
  103.2 0.8 copy-done.2
  104.0 4.0 %merge.1 = f32[64,100]{1,0:T(8,128)} custom-call(s32[512]{0:T(512)} %reshape.15.idx_ref, f32[1024,128]{1,0:T(8,128)} %bitcast.12), custom_call_target="tpu_custom_call" | custom-call | tf_op jit(solution)/shard_map/merge/pallas_call | solution.py:302
  (3 shorter events, 0.0 us)
Async XLA Ops:
  0.0 15.9 %copy-start.3 = (bf16[192,16,4]{0,2,1:T(4,128)(2,1)S(1)}, bf16[192,16,4]{0,2,1:T(4,128)(2,1)}, u32[]{:S(2)}) copy-start(bf16[192,16,4]{0,2,1:T(4,128)(2,1)} %param.6) | copy-start | bytes 73732
  0.0 16.1 %copy-start.4 = (s32[4]{0:T(128)S(1)}, s32[4]{0:T(128)}, u32[]{:S(2)}) copy-start(s32[4]{0:T(128)} %param.9) | copy-start | bytes 52
  0.0 40.9 %collective-permute-start = (s32[4,192,1024]{2,1,0:T(8,128)}, s32[4,192,1024]{2,1,0:T(8,128)}, u32[]{:S(2)}, u32[]{:S(2)}) collective-permute-start(s32[4,192,1024]{2,1,0:T(8,128)} %own_ref.1), channel_id=1, source_target_pairs={{0,1},{1,0},{2,3},{3,2},{4,5},{5,4},{6,7},{7,6},{8,9},{9,8},{10,11... | collective-permute-start | bytes 9437192 | tf_op jit(solution)/shard_map/ppermute | solution.py:321
  0.8 0.9 copy-start.1
  4.3 36.6 %all-to-all-start = ((bf16[64,16,768]{2,1,0:T(8,128)(2,1)}), bf16[64,16,768]{2,1,0:T(8,128)(2,1)S(1)}, u32[]{:S(2)}, u32[]{:S(2)}) async-start(bf16[64,16,768]{2,1,0:T(8,128)(2,1)} %bitcast.4), calls=%async_computation | async-start | bytes 3145728 | tf_op jit(solution)/shard_map/all_to_all | solution.py:323
  40.9 1.9 %copy-start = (s32[4,192,1024]{2,1,0:T(8,128)S(1)}, s32[4,192,1024]{2,1,0:T(8,128)}, u32[]{:S(2)}) copy-start(s32[4,192,1024]{2,1,0:T(8,128)} %own_ref.1) | copy-start | bytes 9437188
  84.7 18.6 %all-to-all-start.1 = ((f32[64,16,128]{2,1,0:T(8,128)}), f32[64,16,128]{2,1,0:T(8,128)S(1)}, u32[]{:S(2)}, u32[]{:S(2)}) async-start(f32[64,16,128]{2,1,0:T(8,128)} %bitcast.6), calls=%async_computation.1 | async-start | bytes 1048576 | tf_op jit(solution)/shard_map/all_to_all | solution.py:329
  103.2 0.8 copy-start.2

commit v2 on v1

--- a/solution.py
+++ b/solution.py
@@ -190,24 +190,49 @@
             x_ref[b0, k * 32 + i] = x[i]
 
 
-def score_kernel(n_cap, sizes_ref, table_ref, q_ref, own_ref, peer_ref, out_ref, d_ref, s_ref, x_ref, z_ref):
-    p = pl.program_id(0)
-    groups, half = own_ref.shape[1:]
-    part_dev = pl.num_programs(0)
-    tiles = half // LANES
+def decode_kernel(table_ref, codes_ref, d_ref, t_ref):
+    groups, half = codes_ref.shape[1:]
 
     @pl.loop(0, groups // 16)
     def _(g):
         rows = pl.ds(pl.multiple_of(g * 16, 16), 16)
         tab = [table_ref[j, rows, :] for j in range(4)]
-        for t in range(2 * tiles):
-            ref = own_ref if t < tiles else peer_ref
-            c = ref[0, rows, (t % tiles) * LANES : (t % tiles + 1) * LANES]
+        for t in range(half // LANES):
+            cols = slice(t * LANES, (t + 1) * LANES)
+            c = codes_ref[0, rows, cols]
             for j in range(4):
                 val = jnp.take_along_axis(tab[j], c, axis=1)
-                d_ref[pl.ds(pl.multiple_of(j * groups + g * 16, 16), 16), t * LANES : (t + 1) * LANES] = val.astype(
-                    jnp.bfloat16
-                )
+                t_ref[pl.ds(pl.multiple_of(j * groups + g * 16, 16), 16), cols] = val.astype(jnp.bfloat16)
+
+    @pl.loop(0, half // 256)
+    def _(t):
+        cols = pl.ds(pl.multiple_of(t * 256, 256), 256)
+        d_ref[0, cols, :] = t_ref[:, cols].T
+
+
+def decode(table, codes):
+    part_dev, groups, half = codes.shape
+    width = groups * 4
+    return pl.pallas_call(
+        decode_kernel,
+        grid=(part_dev,),
+        out_shape=jax.ShapeDtypeStruct((part_dev, half, width), jnp.bfloat16),
+        in_specs=[
+            pl.BlockSpec(memory_space=pltpu.VMEM),
+            pl.BlockSpec((1, groups, half), lambda p: (p, 0, 0)),
+        ],
+        out_specs=pl.BlockSpec((1, half, width), lambda p: (p, 0, 0)),
+        scratch_shapes=[pltpu.VMEM((width, half), jnp.bfloat16)],
+        compiler_params=pltpu.CompilerParams(vmem_limit_bytes=56 << 20),
+        cost_estimate=pl.CostEstimate(flops=10**10, bytes_accessed=20 << 20, transcendentals=0),
+        name="decode",
+    )(table, codes)
+
+
+def score_kernel(n_cap, sizes_ref, q_ref, own_ref, peer_ref, out_ref, s_ref, x_ref, z_ref):
+    p = pl.program_id(0)
+    half = own_ref.shape[1]
+    part_dev = pl.num_programs(0)
 
     all_rows = q_ref.shape[0]
     m = lax.broadcasted_iota(jnp.int32, (256, all_rows), 0)
@@ -216,18 +241,12 @@
     pick = jnp.where(lax.broadcasted_iota(jnp.int32, (256, all_rows), 1) == want, 1.0, 0.0).astype(jnp.bfloat16)
     mine = jnp.dot(pick, q_ref[...], preferred_element_type=jnp.float32).astype(jnp.bfloat16)
 
-    @pl.loop(0, 2 * half // 256)
-    def _(t):
-        cols = pl.ds(pl.multiple_of(t * 256, 256), 256)
-        sc = jnp.dot(mine, d_ref[:, cols], preferred_element_type=jnp.float32)
-        sc = sc.T
-        per_half = half // 256
-        which = t // per_half
-        slot = lax.broadcasted_iota(jnp.int32, (256, LANES), 0) + (t - which * per_half) * 256
-        ok = slot < sizes_ref[which, p]
+    for which, ref in enumerate((own_ref, peer_ref)):
+        sc = lax.dot_general(ref[0], mine, (((1,), (1,)), ((), ())), preferred_element_type=jnp.float32)
+        ok = lax.broadcasted_iota(jnp.int32, (half, LANES), 0) < sizes_ref[which, p]
         for h in range(2):
             blk = jnp.where(ok, sc[:, h * LANES : (h + 1) * LANES], MASKED)
-            s_ref[h, pl.ds(t * 32, 32)] = blk.reshape(32, SUBL, LANES)
+            s_ref[h, pl.ds(which * half // SUBL, half // SUBL)] = blk.reshape(half // SUBL, SUBL, LANES)
 
     for h in range(2):
         sort_block(s_ref, x_ref, h, p * 2 + h)
@@ -248,10 +267,10 @@
                 out_ref[pl.ds(base, 32, stride=16), :] = got[r * 32 : (r + 1) * 32, :]
 
 
-def score(sizes, table, rows, own, peer, n_cap):
-    part_dev, groups, half = own.shape
-    n_rows, width = rows.shape
-    blk = pl.BlockSpec((1, groups, half), lambda p: (p, 0, 0))
+def score(sizes, rows, own, peer, n_cap):
+    part_dev, half, width = own.shape
+    n_rows = rows.shape[0]
+    blk = pl.BlockSpec((1, half, width), lambda p: (p, 0, 0))
     return pl.pallas_call(
         functools.partial(score_kernel, n_cap),
         grid=(part_dev,),
@@ -259,20 +278,18 @@
         in_specs=[
             pl.BlockSpec(memory_space=pltpu.SMEM),
             pl.BlockSpec(memory_space=pltpu.VMEM),
-            pl.BlockSpec(memory_space=pltpu.VMEM),
             blk,
             blk,
         ],
         out_specs=pl.BlockSpec(memory_space=pltpu.VMEM),
         scratch_shapes=[
-            pltpu.VMEM((width, 2 * half), jnp.bfloat16),
             pltpu.VMEM((2, 2 * half // SUBL, SUBL, LANES), jnp.float32),
             pltpu.VMEM((8, RANKS, SUBL, LANES), jnp.float32),
             pltpu.VMEM((RANKS * SUBL, LANES), jnp.float32),
         ],
-        compiler_params=pltpu.CompilerParams(vmem_limit_bytes=48 << 20),
+        compiler_params=pltpu.CompilerParams(vmem_limit_bytes=40 << 20),
         name="score",
-    )(sizes, table, rows, own, peer)
+    )(sizes, rows, own, peer)
 
 
 def merge_kernel(idx_ref, r_ref, out_ref, l_ref):
@@ -305,6 +322,7 @@
         in_specs=[pl.BlockSpec(memory_space=pltpu.SMEM), pl.BlockSpec(memory_space=pltpu.VMEM)],
         out_specs=pl.BlockSpec(memory_space=pltpu.VMEM),
         scratch_shapes=[pltpu.VMEM((total, RANKS), jnp.float32)],
+        compiler_params=pltpu.CompilerParams(vmem_limit_bytes=16 << 20),
         name="merge",
     )(idx, returned)
 
@@ -325,7 +343,7 @@
     ).reshape(n_parts * n_cap, width)
     table = jnp.pad(codebook.astype(jnp.float32).transpose(2, 0, 1), ((0, 0), (0, 0), (0, LANES - n_cent)))
     sizes = jnp.stack([part_sizes - rep * half, part_sizes - (1 - rep) * half])
-    best = score(sizes, table, arrived, codes, peer, n_cap)
+    best = score(sizes, arrived, decode(table, codes), decode(table, peer), n_cap)
     returned = lax.all_to_all(
         best.reshape(n_dev, part_dev * n_cap, RANKS), ("dom", "sub"), split_axis=0, concat_axis=0, tiled=True
     ).reshape(n_parts * n_cap, RANKS)

time: 109 us -> 95.4 us (0.88)
  waiting for transfers between devices: 37.3 us -> 13.3 us
  Pallas kernels: 48.5 us -> 54.1 us
  starting transfers between devices: 16.8 us -> 21.8 us
    all_to_all x1, waiting for transfers between devices: 24.8 us -> 0.01 us  [local(): lax.all_to_all(send.reshape(n_dev, part_dev * n_cap, width), ('dom', 'sub...]
    pallas_call x0 -> x2, Pallas kernels: none -> 24.3 us  [decode(): pl.pallas_call(decode_kernel, grid=(part_dev,), out_shape=jax.ShapeDtypeS...]
    pallas_call x1, Pallas kernels: 41.8 us -> 23.5 us  [score(): pl.pallas_call(functools.partial(score_kernel, n_cap), grid=(part_dev,),...]
    all_to_all x1, starting transfers between devices: 5.33 us -> 10.3 us  [local(): lax.all_to_all(best.reshape(n_dev, part_dev * n_cap, RANKS), ('dom', 'sub...]
    unnamed x12 -> x10, local copies, waits for them, and re-layouts: 4.55 us -> 4.66 us
  transfers between devices with their start and end apart: 3 -> 3, of which waited for: 2 -> 1; matrix products, arithmetic and copies ran while one was open for 2% -> 2% of each run, Pallas kernels for 2% -> 28%
where the time goes in v2:
time: 95.4 us; the launch traced here: 94.9 us
  Pallas kernels  54.1 us (57%)
  starting transfers between devices  21.8 us (23%)
  waiting for transfers between devices  13.3 us (14%)
  local copies, waits for them, and re-layouts  4.8 us (5%)
    pallas_call x2, Pallas kernels, decode(): pl.pallas_call(decode_kernel, grid=(part_dev,), out_shape=jax.ShapeDtypeS...  24.3 us
    pallas_call x1, Pallas kernels, score(): pl.pallas_call(functools.partial(score_kernel, n_cap), grid=(part_dev,),...  23.5 us
    all_to_all x1, waiting for transfers between devices, local(): lax.all_to_all(best.reshape(n_dev, part_dev * n_cap, RANKS), ('dom', 'sub...  13.3 us
    all_to_all x1, starting transfers between devices, local(): lax.all_to_all(send.reshape(n_dev, part_dev * n_cap, width), ('dom', 'sub...  11.5 us
    all_to_all x1, starting transfers between devices, local(): lax.all_to_all(best.reshape(n_dev, part_dev * n_cap, RANKS), ('dom', 'sub...  10.3 us
    unnamed x10, local copies, waits for them, and re-layouts  4.66 us
    pallas_call x1, Pallas kernels, merge(): pl.pallas_call(merge_kernel, out_shape=jax.ShapeDtypeStruct((n_rows, TOPK...  3.58 us
    pallas_call x1, Pallas kernels, prep(): pl.pallas_call(functools.partial(prep_kernel, n_cap), out_shape=(jax.Shap...  2.64 us
  transfers between devices with their start and end apart: 3, of which 1 were waited for; matrix products, arithmetic and copies ran while one was open for 2% of the time, Pallas kernels for 28%

profile of v2, /device:TPU:0, one launch (start us, length us, event | category | flops | bytes accessed | tf_op | source)
XLA Modules:
  0.0 94.9 jit_solution(2872560817460973758)
XLA Ops:
  0.0 0.0 copy-start.2
  0.0 0.0 copy-start.3
  0.0 0.0 collective-permute-start
  0.0 0.8 copy.8.probes_ref
  0.8 0.0 copy-start.1
  0.8 0.9 copy-done.1
  1.7 2.6 %prep.1 = (bf16[1024,768]{1,0:T(8,128)(2,1)}, s32[64,8]{1,0:T(8,128)S(1)}) custom-call(bf16[64,768]{1,0:T(8,128)(2,1)S(1)} %copy-done.1, s32[64,8]{1,0:T(8,128)S(1)} %copy.8.probes_ref), custom_call_target="tpu_custom_call" | custom-call | tf_op jit(solution)/shard_map/prep/pallas_call | solution.py:92
  4.3 11.5 %all-to-all-start = ((bf16[64,16,768]{2,1,0:T(8,128)(2,1)}), bf16[64,16,768]{2,1,0:T(8,128)(2,1)S(1)}, u32[]{:S(2)}, u32[]{:S(2)}) async-start(bf16[64,16,768]{2,1,0:T(8,128)(2,1)} %bitcast.3), calls=%async_computation | async-start | bytes 3145728 | tf_op jit(solution)/shard_map/all_to_all | solution.py:341
  15.9 0.0 copy-done.2
  15.9 0.2 copy.10
  16.1 0.0 copy-done.3
  16.1 0.8 pad_convert_fusion.table_ref
  16.9 12.2 %decode.2.own_ref = bf16[4,1024,768]{2,1,0:T(8,128)(2,1)} custom-call(f32[4,192,128]{2,1,0:T(8,128)} %pad_convert_fusion.table_ref, s32[4,192,1024]{2,1,0:T(8,128)} %codes_ref.1), custom_call_target="tpu_custom_call" | custom-call | flops 10000000000 | bytes 20971520 | tf_op jit(solution)/shard_map/decode/pallas_call | solution.py:216
  29.0 0.0 collective-permute-done.codes_ref
  29.0 12.2 %decode.3.peer_ref = bf16[4,1024,768]{2,1,0:T(8,128)(2,1)} custom-call(f32[4,192,128]{2,1,0:T(8,128)} %pad_convert_fusion.table_ref, s32[4,192,1024]{2,1,0:T(8,128)} %collective-permute-done.codes_ref), custom_call_target="tpu_custom_call" | custom-call | flops 10000000000 | bytes 20971520 | tf_op jit(solution)/shard_map/decode/pallas_call | solution.py:216
  41.2 0.0 all-to-all-done
  41.2 0.0 copy-start
  41.2 2.8 %copy-done = bf16[4,1024,768]{2,1,0:T(8,128)(2,1)S(1)} copy-done((bf16[4,1024,768]{2,1,0:T(8,128)(2,1)S(1)}, bf16[4,1024,768]{2,1,0:T(8,128)(2,1)}, u32[]{:S(2)}) %copy-start) | copy-done | bytes 6291480
  44.0 23.5 %score.1 = f32[1024,128]{1,0:T(8,128)} custom-call(s32[2,4]{1,0:T(2,128)S(1)} %pad_add_fusion.sizes_ref, bf16[1024,768]{1,0:T(8,128)(2,1)S(1)} %bitcast.10, bf16[4,1024,768]{2,1,0:T(8,128)(2,1)S(1)} %copy-done, bf16[4,1024,768]{2,1,0:T(8,128)(2,1)} %decode.3.peer_ref), custom_call_target="tpu_custom_call" | custom-call | tf_op jit(solution)/shard_map/score/pallas_call | solution.py:274
  67.5 10.3 %all-to-all-start.1 = ((f32[64,16,128]{2,1,0:T(8,128)}), f32[64,16,128]{2,1,0:T(8,128)S(1)}, u32[]{:S(2)}, u32[]{:S(2)}) async-start(f32[64,16,128]{2,1,0:T(8,128)} %bitcast.6), calls=%async_computation.1 | async-start | bytes 1048576 | tf_op jit(solution)/shard_map/all_to_all | solution.py:347
  77.9 0.1 copy.9
  77.9 0.1 reshape.15.idx_ref
  78.0 13.3 %all-to-all-done.1 = f32[64,16,128]{2,1,0:T(8,128)S(1)} async-done(((f32[64,16,128]{2,1,0:T(8,128)}), f32[64,16,128]{2,1,0:T(8,128)S(1)}, u32[]{:S(2)}, u32[]{:S(2)}) %all-to-all-start.1) | async-done | bytes 524320 | tf_op jit(solution)/shard_map/all_to_all | solution.py:347
  91.3 3.6 %merge.1 = f32[64,100]{1,0:T(8,128)} custom-call(s32[512]{0:T(512)S(1)} %reshape.15.idx_ref, f32[1024,128]{1,0:T(8,128)S(1)} %bitcast.11), custom_call_target="tpu_custom_call" | custom-call | tf_op jit(solution)/shard_map/merge/pallas_call | solution.py:319
  (2 shorter events, 0.0 us)
Async XLA Ops:
  0.0 15.9 %copy-start.2 = (bf16[192,16,4]{0,2,1:T(4,128)(2,1)S(1)}, bf16[192,16,4]{0,2,1:T(4,128)(2,1)}, u32[]{:S(2)}) copy-start(bf16[192,16,4]{0,2,1:T(4,128)(2,1)} %param.6) | copy-start | bytes 73732
  0.0 16.1 %copy-start.3 = (s32[4]{0:T(128)S(1)}, s32[4]{0:T(128)}, u32[]{:S(2)}) copy-start(s32[4]{0:T(128)} %param.9) | copy-start | bytes 52
  0.0 29.0 %collective-permute-start = (s32[4,192,1024]{2,1,0:T(8,128)}, s32[4,192,1024]{2,1,0:T(8,128)}, u32[]{:S(2)}, u32[]{:S(2)}) collective-permute-start(s32[4,192,1024]{2,1,0:T(8,128)} %codes_ref.1), channel_id=1, source_target_pairs={{0,1},{1,0},{2,3},{3,2},{4,5},{5,4},{6,7},{7,6},{8,9},{9,8},{10,11... | collective-permute-start | bytes 9437192 | tf_op jit(solution)/shard_map/ppermute | solution.py:339
  0.8 0.9 copy-start.1
  4.3 36.9 %all-to-all-start = ((bf16[64,16,768]{2,1,0:T(8,128)(2,1)}), bf16[64,16,768]{2,1,0:T(8,128)(2,1)S(1)}, u32[]{:S(2)}, u32[]{:S(2)}) async-start(bf16[64,16,768]{2,1,0:T(8,128)(2,1)} %bitcast.3), calls=%async_computation | async-start | bytes 3145728 | tf_op jit(solution)/shard_map/all_to_all | solution.py:341
  41.2 2.8 %copy-start = (bf16[4,1024,768]{2,1,0:T(8,128)(2,1)S(1)}, bf16[4,1024,768]{2,1,0:T(8,128)(2,1)}, u32[]{:S(2)}) copy-start(bf16[4,1024,768]{2,1,0:T(8,128)(2,1)} %decode.2.own_ref) | copy-start | bytes 18874372
  67.5 23.8 %all-to-all-start.1 = ((f32[64,16,128]{2,1,0:T(8,128)}), f32[64,16,128]{2,1,0:T(8,128)S(1)}, u32[]{:S(2)}, u32[]{:S(2)}) async-start(f32[64,16,128]{2,1,0:T(8,128)} %bitcast.6), calls=%async_computation.1 | async-start | bytes 1048576 | tf_op jit(solution)/shard_map/all_to_all | solution.py:347

commit v3 on v1

--- a/solution.py
+++ b/solution.py
@@ -57,9 +57,18 @@
     return x
 
 
-def prep_kernel(n_cap, q_ref, probes_ref, send_ref, idx_ref):
+MESH = pl.DeviceIdType.MESH
+
+
+def device_of(t):
+    n_sub = lax.axis_size("sub")
+    return {"dom": t // n_sub, "sub": t % n_sub}
+
+
+def route(n_cap, q_ref, probes_ref, send_ref, idx_ref):
     rows, width = q_ref.shape
-    slots = send_ref.shape[0]
+    n_dev, chip_slots, _ = send_ref.shape
+    slots = n_dev * chip_slots
     n = lax.broadcasted_iota(jnp.int32, (rows, slots), 1)
     part = n // n_cap
     rank_of = (n % n_cap).astype(jnp.float32)
@@ -85,21 +94,139 @@
     picked = lax.dot_general(
         chosen.astype(jnp.bfloat16), moved, (((0,), (0,)), ((), ())), preferred_element_type=jnp.float32
     )
-    send_ref[...] = picked.astype(jnp.bfloat16)
-
-
-def prep(queries, probes, n_slots, n_cap):
+    send_ref[...] = picked.astype(jnp.bfloat16).reshape(send_ref.shape)
+
+
+def decode(table_ref, codes_ref, p, t_ref, d_ref, slot):
+    groups, half = codes_ref.shape[1:]
+
+    @pl.loop(0, groups // 16)
+    def _(g):
+        rows = pl.ds(pl.multiple_of(g * 16, 16), 16)
+        tab = [table_ref[j, rows, :] for j in range(4)]
+        for t in range(half // LANES):
+            cols = slice(t * LANES, (t + 1) * LANES)
+            c = codes_ref[p, rows, cols]
+            for j in range(4):
+                val = jnp.take_along_axis(tab[j], c, axis=1)
+                t_ref[pl.ds(pl.multiple_of(j * groups + g * 16, 16), 16), cols] = val.astype(jnp.bfloat16)
+
+    @pl.loop(0, half // 256)
+    def _(t):
+        cols = pl.ds(pl.multiple_of(t * 256, 256), 256)
+        d_ref[slot, cols, :] = t_ref[:, cols].T
+
+
+def fetch_kernel(
+    n_cap, q_ref, probes_ref, table_ref, codes_ref, rows_ref, idx_ref, d_out,
+    send_ref, own_ref, peer_ref, t_ref, d_ref,
+    in_sem, out_sem, code_send, code_recv, row_send, row_recv, local_sem,
+):
+    n_dev = send_ref.shape[0]
+    part_dev = codes_ref.shape[0]
+    me = lax.axis_index("dom") * lax.axis_size("sub") + lax.axis_index("sub")
+    other = {"rep": 1 - lax.axis_index("rep")}
+
+    loads = [pltpu.make_async_copy(codes_ref.at[p], own_ref.at[p], in_sem.at[p]) for p in range(part_dev)]
+    for c in loads:
+        c.start()
+    barrier = pltpu.get_barrier_semaphore()
+    pl.semaphore_signal(barrier, inc=1, device_id=other, device_id_type=MESH)
+
+    @pl.loop(1, n_dev)
+    def _(k):
+        pl.semaphore_signal(barrier, inc=1, device_id=device_of((me + k) % n_dev), device_id_type=MESH)
+
+    route(n_cap, q_ref, probes_ref, send_ref, idx_ref)
+    pl.semaphore_wait(barrier, n_dev)
+
+    def row_copy(k):
+        t = (me + k) % n_dev
+        return pltpu.make_async_remote_copy(
+            src_ref=send_ref.at[t],
+            dst_ref=rows_ref.at[me],
+            send_sem=row_send.at[k],
+            recv_sem=row_recv.at[k],
+            device_id=device_of(t),
+            device_id_type=MESH,
+        )
+
+    @pl.loop(1, n_dev)
+    def _(k):
+        row_copy(k).start()
+
+    swaps = [
+        pltpu.make_async_remote_copy(
+            src_ref=codes_ref.at[p],
+            dst_ref=peer_ref.at[p],
+            send_sem=code_send.at[p],
+            recv_sem=code_recv.at[p],
+            device_id=other,
+            device_id_type=MESH,
+        )
+        for p in range(part_dev)
+    ]
+    for c in swaps:
+        c.start()
+    keep = pltpu.make_async_copy(send_ref.at[me], rows_ref.at[me], local_sem)
+    keep.start()
+
+    writes = []
+    for which, ref in enumerate((own_ref, peer_ref)):
+        for p in range(part_dev):
+            n = which * part_dev + p
+            if which == 0:
+                loads[p].wait()
+            else:
+                swaps[p].wait()
+            if n >= 2:
+                writes[n - 2].wait()
+            decode(table_ref, ref, p, t_ref, d_ref, n % 2)
+            w = pltpu.make_async_copy(d_ref.at[n % 2], d_out.at[which, p], out_sem.at[n])
+            w.start()
+            writes.append(w)
+    keep.wait()
+
+    @pl.loop(1, n_dev)
+    def _(k):
+        row_copy(k).wait()
+
+    writes[-2].wait()
+    writes[-1].wait()
+
+
+def fetch(queries, probes, table, codes, n_dev, n_cap):
+    part_dev, groups, half = codes.shape
+    width = queries.shape[1]
+    vmem = pl.BlockSpec(memory_space=pltpu.VMEM)
+    hbm = pl.BlockSpec(memory_space=pl.ANY)
+    dma = pltpu.SemaphoreType.DMA
     return pl.pallas_call(
-        functools.partial(prep_kernel, n_cap),
+        functools.partial(fetch_kernel, n_cap),
         out_shape=(
-            jax.ShapeDtypeStruct((n_slots, queries.shape[1]), jnp.bfloat16),
+            jax.ShapeDtypeStruct((n_dev, part_dev * n_cap, width), jnp.bfloat16),
             jax.ShapeDtypeStruct(probes.shape, jnp.int32),
+            jax.ShapeDtypeStruct((2, part_dev, half, width), jnp.bfloat16),
         ),
-        in_specs=[pl.BlockSpec(memory_space=pltpu.VMEM)] * 2,
-        out_specs=[pl.BlockSpec(memory_space=pltpu.VMEM)] * 2,
-        compiler_params=pltpu.CompilerParams(vmem_limit_bytes=40 << 20),
-        name="prep",
-    )(queries, probes)
+        in_specs=[vmem, vmem, vmem, hbm],
+        out_specs=[hbm, vmem, hbm],
+        scratch_shapes=[
+            pltpu.VMEM((n_dev, part_dev * n_cap, width), jnp.bfloat16),
+            pltpu.VMEM(codes.shape, jnp.int32),
+            pltpu.VMEM(codes.shape, jnp.int32),
+            pltpu.VMEM((width, half), jnp.bfloat16),
+            pltpu.VMEM((2, half, width), jnp.bfloat16),
+            dma((part_dev,)),
+            dma((2 * part_dev,)),
+            dma((part_dev,)),
+            dma((part_dev,)),
+            dma((n_dev,)),
+            dma((n_dev,)),
+            dma,
+        ],
+        compiler_params=pltpu.CompilerParams(collective_id=0, has_side_effects=True, vmem_limit_bytes=56 << 20),
+        name="fetch",
+    )(queries, probes, table, codes)
 
 
 def sort_block(s_ref, x_ref, b, h):
@@ -190,24 +317,10 @@
             x_ref[b0, k * 32 + i] = x[i]
 
 
-def score_kernel(n_cap, sizes_ref, table_ref, q_ref, own_ref, peer_ref, out_ref, d_ref, s_ref, x_ref, z_ref):
+def score_kernel(n_cap, sizes_ref, q_ref, own_ref, peer_ref, out_ref, s_ref, x_ref, z_ref):
     p = pl.program_id(0)
-    groups, half = own_ref.shape[1:]
+    half = own_ref.shape[2]
     part_dev = pl.num_programs(0)
-    tiles = half // LANES
-
-    @pl.loop(0, groups // 16)
-    def _(g):
-        rows = pl.ds(pl.multiple_of(g * 16, 16), 16)
-        tab = [table_ref[j, rows, :] for j in range(4)]
-        for t in range(2 * tiles):
-            ref = own_ref if t < tiles else peer_ref
-            c = ref[0, rows, (t % tiles) * LANES : (t % tiles + 1) * LANES]
-            for j in range(4):
-                val = jnp.take_along_axis(tab[j], c, axis=1)
-                d_ref[pl.ds(pl.multiple_of(j * groups + g * 16, 16), 16), t * LANES : (t + 1) * LANES] = val.astype(
-                    jnp.bfloat16
-                )
 
     all_rows = q_ref.shape[0]
     m = lax.broadcasted_iota(jnp.int32, (256, all_rows), 0)
@@ -216,18 +329,12 @@
     pick = jnp.where(lax.broadcasted_iota(jnp.int32, (256, all_rows), 1) == want, 1.0, 0.0).astype(jnp.bfloat16)
     mine = jnp.dot(pick, q_ref[...], preferred_element_type=jnp.float32).astype(jnp.bfloat16)
 
-    @pl.loop(0, 2 * half // 256)
-    def _(t):
-        cols = pl.ds(pl.multiple_of(t * 256, 256), 256)
-        sc = jnp.dot(mine, d_ref[:, cols], preferred_element_type=jnp.float32)
-        sc = sc.T
-        per_half = half // 256
-        which = t // per_half
-        slot = lax.broadcasted_iota(jnp.int32, (256, LANES), 0) + (t - which * per_half) * 256
-        ok = slot < sizes_ref[which, p]
+    for which, ref in enumerate((own_ref, peer_ref)):
+        sc = lax.dot_general(ref[0, 0], mine, (((1,), (1,)), ((), ())), preferred_element_type=jnp.float32)
+        ok = lax.broadcasted_iota(jnp.int32, (half, LANES), 0) < sizes_ref[which, p]
         for h in range(2):
             blk = jnp.where(ok, sc[:, h * LANES : (h + 1) * LANES], MASKED)
-            s_ref[h, pl.ds(t * 32, 32)] = blk.reshape(32, SUBL, LANES)
+            s_ref[h, pl.ds(which * half // SUBL, half // SUBL)] = blk.reshape(half // SUBL, SUBL, LANES)
 
     for h in range(2):
         sort_block(s_ref, x_ref, h, p * 2 + h)
@@ -248,10 +355,9 @@
                 out_ref[pl.ds(base, 32, stride=16), :] = got[r * 32 : (r + 1) * 32, :]
 
 
-def score(sizes, table, rows, own, peer, n_cap):
-    part_dev, groups, half = own.shape
-    n_rows, width = rows.shape
-    blk = pl.BlockSpec((1, groups, half), lambda p: (p, 0, 0))
+def score(sizes, rows, decoded, n_cap):
+    _, part_dev, half, width = decoded.shape
+    n_rows = rows.shape[0]
     return pl.pallas_call(
         functools.partial(score_kernel, n_cap),
         grid=(part_dev,),
@@ -259,20 +365,18 @@
         in_specs=[
             pl.BlockSpec(memory_space=pltpu.SMEM),
             pl.BlockSpec(memory_space=pltpu.VMEM),
-            pl.BlockSpec(memory_space=pltpu.VMEM),
-            blk,
-            blk,
+            pl.BlockSpec((1, 1, half, width), lambda p: (0, p, 0, 0)),
+            pl.BlockSpec((1, 1, half, width), lambda p: (1, p, 0, 0)),
         ],
         out_specs=pl.BlockSpec(memory_space=pltpu.VMEM),
         scratch_shapes=[
-            pltpu.VMEM((width, 2 * half), jnp.bfloat16),
             pltpu.VMEM((2, 2 * half // SUBL, SUBL, LANES), jnp.float32),
             pltpu.VMEM((8, RANKS, SUBL, LANES), jnp.float32),
             pltpu.VMEM((RANKS * SUBL, LANES), jnp.float32),
         ],
-        compiler_params=pltpu.CompilerParams(vmem_limit_bytes=48 << 20),
+        compiler_params=pltpu.CompilerParams(vmem_limit_bytes=46 << 20),
         name="score",
-    )(sizes, table, rows, own, peer)
+    )(sizes, rows, decoded, decoded)
 
 
 def merge_kernel(idx_ref, r_ref, out_ref, l_ref):
@@ -305,6 +409,7 @@
         in_specs=[pl.BlockSpec(memory_space=pltpu.SMEM), pl.BlockSpec(memory_space=pltpu.VMEM)],
         out_specs=pl.BlockSpec(memory_space=pltpu.VMEM),
         scratch_shapes=[pltpu.VMEM((total, RANKS), jnp.float32)],
+        compiler_params=pltpu.CompilerParams(vmem_limit_bytes=16 << 20),
         name="merge",
     )(idx, returned)
 
@@ -318,14 +423,10 @@
     n_cent = codebook.shape[1]
     n_parts = part_dev * n_dev
     n_cap = max(2, 2 * own_rows * n_probe // n_parts)
-    peer = lax.ppermute(codes, "rep", [(0, 1), (1, 0)])
-    send, idx = prep(queries, probes, n_parts * n_cap, n_cap)
-    arrived = lax.all_to_all(
-        send.reshape(n_dev, part_dev * n_cap, width), ("dom", "sub"), split_axis=0, concat_axis=0, tiled=True
-    ).reshape(n_parts * n_cap, width)
     table = jnp.pad(codebook.astype(jnp.float32).transpose(2, 0, 1), ((0, 0), (0, 0), (0, LANES - n_cent)))
     sizes = jnp.stack([part_sizes - rep * half, part_sizes - (1 - rep) * half])
-    best = score(sizes, table, arrived, codes, peer, n_cap)
+    arrived, idx, decoded = fetch(queries, probes, table, codes, n_dev, n_cap)
+    best = score(sizes, arrived.reshape(n_parts * n_cap, width), decoded, n_cap)
     returned = lax.all_to_all(
         best.reshape(n_dev, part_dev * n_cap, RANKS), ("dom", "sub"), split_axis=0, concat_axis=0, tiled=True
     ).reshape(n_parts * n_cap, RANKS)

time: 109 us -> 88.2 us (0.81)
  waiting for transfers between devices: 37.3 us -> 12 us
  Pallas kernels: 48.5 us -> 62.2 us
  starting transfers between devices: 16.8 us -> 8.32 us
  local copies, waits for them, and re-layouts: 5.28 us -> 3.85 us
  other arithmetic: 0.05 us -> 1.45 us
    pallas_call x1, Pallas kernels: 2.65 us -> 34.6 us  [fetch(): pl.pallas_call(functools.partial(fetch_kernel, n_cap), out_shape=(jax.Sha...]
    all_to_all x1 -> x0, waiting for transfers between devices: 24.8 us -> none  [local(): lax.all_to_all(send.reshape(n_dev, part_dev * n_cap, width), ('dom', 'sub...]
    pallas_call x1, Pallas kernels: 41.8 us -> 24 us  [score(): pl.pallas_call(functools.partial(score_kernel, n_cap), grid=(part_dev,),...]
    all_to_all x1 -> x0, starting transfers between devices: 11.5 us -> none  [local(): lax.all_to_all(send.reshape(n_dev, part_dev * n_cap, width), ('dom', 'sub...]
    all_to_all x1, starting transfers between devices: 5.33 us -> 8.32 us  [local(): lax.all_to_all(best.reshape(n_dev, part_dev * n_cap, RANKS), ('dom', 'sub...]
    unnamed x12 -> x6, local copies, waits for them, and re-layouts: 4.55 us -> 3.71 us
  transfers between devices with their start and end apart: 3 -> 1, of which waited for: 2 -> 1; matrix products, arithmetic and copies ran while one was open for 2% -> 0% of each run, Pallas kernels for 2% -> 0%
where the time goes in v3:
time: 88.2 us; the launch traced here: 87.9 us
  Pallas kernels  62.2 us (71%)
  waiting for transfers between devices  12 us (14%)
  starting transfers between devices  8.32 us (9%)
  local copies, waits for them, and re-layouts  3.85 us (4%)
  other arithmetic  1.45 us (2%)
    pallas_call x1, Pallas kernels, fetch(): pl.pallas_call(functools.partial(fetch_kernel, n_cap), out_shape=(jax.Sha...  34.6 us
    pallas_call x1, Pallas kernels, score(): pl.pallas_call(functools.partial(score_kernel, n_cap), grid=(part_dev,),...  24 us
    all_to_all x1, waiting for transfers between devices, local(): lax.all_to_all(best.reshape(n_dev, part_dev * n_cap, RANKS), ('dom', 'sub...  12 us
    all_to_all x1, starting transfers between devices, local(): lax.all_to_all(best.reshape(n_dev, part_dev * n_cap, RANKS), ('dom', 'sub...  8.32 us
    unnamed x6, local copies, waits for them, and re-layouts  3.71 us
    pallas_call x1, Pallas kernels, merge(): pl.pallas_call(merge_kernel, out_shape=jax.ShapeDtypeStruct((n_rows, TOPK...  3.58 us
  transfers between devices with their start and end apart: 1, of which 1 were waited for; matrix products, arithmetic and copies ran while one was open for 0% of the time, Pallas kernels for 0%

profile of v3, /device:TPU:0, one launch (start us, length us, event | category | flops | bytes accessed | tf_op | source)
XLA Modules:
  0.0 87.9 jit_solution(8471350355792666735)
XLA Ops:
  0.0 1.4 %copy.9.probes_ref = s32[64,8]{1,0:T(8,128)} copy(s32[64,8]{0,1:T(8,128)} %param.7) | data formatting | bytes 4096 | tf_op args[2]
  1.4 0.9 %copy.8 = bf16[192,16,4]{1,0,2:T(8,128)(2,1)S(1)} copy(bf16[192,16,4]{0,2,1:T(4,128)(2,1)} %param.6) | data formatting | bytes 49152 | tf_op args[1]
  2.3 0.8 pad_convert_fusion.table_ref
  3.1 0.7 subtract_bitcast_fusion.1
  3.8 34.6 %fetch.1 = (bf16[64,16,768]{2,1,0:T(8,128)(2,1)}, s32[64,8]{1,0:T(8,128)}, bf16[2,4,1024,768]{3,2,1,0:T(8,128)(2,1)}) custom-call(bf16[64,768]{1,0:T(8,128)(2,1)} %q_ref.1, s32[64,8]{1,0:T(8,128)} %copy.9.probes_ref, f32[4,192,128]{2,1,0:T(8,128)} %pad_convert_fusion.table_ref, s32[4,192,1024]{2,1,0:T(8,128)} %codes_ref.1), custom_call_target="tpu_custom_call" | custom-call | tf_op jit(solution)/shard_map/fetch/pallas_call | solution.py:204
  38.4 0.0 copy-start
  38.4 1.4 %copy-done = bf16[64,16,768]{2,1,0:T(8,128)(2,1)S(1)} copy-done((bf16[64,16,768]{2,1,0:T(8,128)(2,1)S(1)}, bf16[64,16,768]{2,1,0:T(8,128)(2,1)}, u32[]{:S(2)}) %copy-start) | copy-done | bytes 1572888
  39.8 0.0 copy-start.1
  39.8 24.0 %score.1 = f32[1024,128]{1,0:T(8,128)} custom-call(s32[2,4]{1,0:T(2,128)S(1)} %pad_add_fusion.sizes_ref, bf16[1024,768]{1,0:T(8,128)(2,1)S(1)} %bitcast.10, bf16[2,4,1024,768]{3,2,1,0:T(8,128)(2,1)} %get-tuple-element.10.own_ref.peer_ref, bf16[2,4,1024,768]{3,2,1,0:T(8,128)(2,1)} %get-tuple-element.10.own_ref.peer_ref), custom_call_target="tpu_custom_call" | custom-call | tf_op jit(solution)/shard_map/score/pallas_call | solution.py:361
  63.8 8.3 %all-to-all-start = ((f32[64,16,128]{2,1,0:T(8,128)}), f32[64,16,128]{2,1,0:T(8,128)S(1)}, u32[]{:S(2)}, u32[]{:S(2)}) async-start(f32[64,16,128]{2,1,0:T(8,128)} %bitcast.5), calls=%async_computation | async-start | bytes 1048576 | tf_op jit(solution)/shard_map/all_to_all | solution.py:430
  72.1 0.0 copy-done.1
  72.1 0.1 copy.10
  72.2 0.1 reshape.12.idx_ref
  72.3 12.0 %all-to-all-done = f32[64,16,128]{2,1,0:T(8,128)S(1)} async-done(((f32[64,16,128]{2,1,0:T(8,128)}), f32[64,16,128]{2,1,0:T(8,128)S(1)}, u32[]{:S(2)}, u32[]{:S(2)}) %all-to-all-start) | async-done | bytes 524320 | tf_op jit(solution)/shard_map/all_to_all | solution.py:430
  84.3 3.6 %merge.1 = f32[64,100]{1,0:T(8,128)} custom-call(s32[512]{0:T(512)S(1)} %reshape.12.idx_ref, f32[1024,128]{1,0:T(8,128)S(1)} %bitcast.9), custom_call_target="tpu_custom_call" | custom-call | tf_op jit(solution)/shard_map/merge/pallas_call | solution.py:406
  (1 shorter events, 0.0 us)
Async XLA Ops:
  38.4 1.4 %copy-start = (bf16[64,16,768]{2,1,0:T(8,128)(2,1)S(1)}, bf16[64,16,768]{2,1,0:T(8,128)(2,1)}, u32[]{:S(2)}) copy-start(bf16[64,16,768]{2,1,0:T(8,128)(2,1)} %get-tuple-element.9) | copy-start | bytes 4718596
  39.8 32.3 %copy-start.1 = (s32[64,8]{1,0:T(8,128)S(1)}, s32[64,8]{1,0:T(8,128)}, u32[]{:S(2)}) copy-start(s32[64,8]{1,0:T(8,128)} %get-tuple-element.8) | copy-start | bytes 6148
  63.8 20.5 %all-to-all-start = ((f32[64,16,128]{2,1,0:T(8,128)}), f32[64,16,128]{2,1,0:T(8,128)S(1)}, u32[]{:S(2)}, u32[]{:S(2)}) async-start(f32[64,16,128]{2,1,0:T(8,128)} %bitcast.5), calls=%async_computation | async-start | bytes 1048576 | tf_op jit(solution)/shard_map/all_to_all | solution.py:430

commit v4 on v3

--- a/solution.py
+++ b/solution.py
@@ -69,32 +69,39 @@
     rows, width = q_ref.shape
     n_dev, chip_slots, _ = send_ref.shape
     slots = n_dev * chip_slots
-    n = lax.broadcasted_iota(jnp.int32, (rows, slots), 1)
+    n = lax.broadcasted_iota(jnp.int32, (slots, rows), 0)
     part = n // n_cap
     rank_of = (n % n_cap).astype(jnp.float32)
-    probes = probes_ref[...]
-    named = part == probes[:, 0:1]
-    for k in range(1, probes.shape[1]):
-        named = named | (part == probes[:, k : k + 1])
+    n_probe = probes_ref.shape[0]
+    hits = [part == probes_ref[k : k + 1, :] for k in range(n_probe)]
+    named = hits[0]
+    for k in range(1, n_probe):
+        named = named | hits[k]
     before = (
-        lax.broadcasted_iota(jnp.int32, (rows, rows), 0) > lax.broadcasted_iota(jnp.int32, (rows, rows), 1)
+        lax.broadcasted_iota(jnp.int32, (rows, rows), 0) < lax.broadcasted_iota(jnp.int32, (rows, rows), 1)
     ).astype(jnp.float32).astype(jnp.bfloat16)
-    rank = jnp.dot(before, named.astype(jnp.float32).astype(jnp.bfloat16), preferred_element_type=jnp.float32)
-    chosen = jnp.where(named & (rank == rank_of), 1.0, 0.0)
-    nf = n.astype(jnp.float32)
-    for k in range(probes.shape[1]):
-        hit = jnp.where(part == probes[:, k : k + 1], chosen, 0.0)
-        idx_ref[:, k : k + 1] = jnp.sum(hit * nf, axis=1, keepdims=True).astype(jnp.int32)
+    rank = jnp.dot(named.astype(jnp.float32).astype(jnp.bfloat16), before, preferred_element_type=jnp.float32)
+    chosen = named & (rank == rank_of)
+    nf = jnp.where(chosen, n, 0)
+    for k in range(n_probe):
+        idx_ref[k : k + 1, :] = jnp.sum(jnp.where(hits[k], nf, 0), axis=0, keepdims=True)
     a = lax.broadcasted_iota(jnp.int32, (width, width), 0)
     b = lax.broadcasted_iota(jnp.int32, (width, width), 1)
     groups = width // 4
     j = (b >= groups).astype(jnp.int32) + (b >= 2 * groups).astype(jnp.int32) + (b >= 3 * groups).astype(jnp.int32)
     perm = jnp.where(a == (b - groups * j) * 4 + j, 1.0, 0.0).astype(jnp.bfloat16)
     moved = jnp.dot(q_ref[...], perm, preferred_element_type=jnp.float32).astype(jnp.bfloat16)
-    picked = lax.dot_general(
-        chosen.astype(jnp.bfloat16), moved, (((0,), (0,)), ((), ())), preferred_element_type=jnp.float32
-    )
+    pick = jnp.where(chosen, 1.0, 0.0).astype(jnp.bfloat16)
+    picked = jnp.dot(pick, moved, preferred_element_type=jnp.float32)
     send_ref[...] = picked.astype(jnp.bfloat16).reshape(send_ref.shape)
+
+
+def fill_table(book_ref, table_ref):
+    n_cent, n_feat, groups = book_ref.shape
+    for j in range(n_feat):
+        plane = book_ref[:, j, :].astype(jnp.float32)
+        wide = jnp.concatenate([plane, jnp.zeros((LANES - n_cent, groups), jnp.float32)], axis=0)
+        table_ref[j] = wide.T
 
 
 def decode(table_ref, codes_ref, p, t_ref, d_ref, slot):
@@ -118,8 +125,8 @@
 
 
 def fetch_kernel(
-    n_cap, q_ref, probes_ref, table_ref, codes_ref, rows_ref, idx_ref, d_out,
-    send_ref, own_ref, peer_ref, t_ref, d_ref,
+    n_cap, q_ref, probes_ref, book_ref, codes_ref, rows_ref, idx_ref, d_out,
+    send_ref, own_ref, peer_ref, t_ref, d_ref, table_ref,
     in_sem, out_sem, code_send, code_recv, row_send, row_recv, local_sem,
 ):
     n_dev = send_ref.shape[0]
@@ -170,6 +177,7 @@
         c.start()
     keep = pltpu.make_async_copy(send_ref.at[me], rows_ref.at[me], local_sem)
     keep.start()
+    fill_table(book_ref, table_ref)
 
     writes = []
     for which, ref in enumerate((own_ref, peer_ref)):
@@ -195,7 +203,7 @@
     writes[-1].wait()
 
 
-def fetch(queries, probes, table, codes, n_dev, n_cap):
+def fetch(queries, probes, book, codes, n_dev, n_cap):
     part_dev, groups, half = codes.shape
     width = queries.shape[1]
     vmem = pl.BlockSpec(memory_space=pltpu.VMEM)
@@ -208,7 +216,7 @@
             jax.ShapeDtypeStruct(probes.shape, jnp.int32),
             jax.ShapeDtypeStruct((2, part_dev, half, width), jnp.bfloat16),
         ),
-        in_specs=[vmem, vmem, vmem, hbm],
+        in_specs=[vmem, vmem, vmem, pl.BlockSpec(memory_space=pltpu.HBM)],
         out_specs=[hbm, vmem, hbm],
         scratch_shapes=[
             pltpu.VMEM((n_dev, part_dev * n_cap, width), jnp.bfloat16),
@@ -216,6 +224,7 @@
             pltpu.VMEM(codes.shape, jnp.int32),
             pltpu.VMEM((width, half), jnp.bfloat16),
             pltpu.VMEM((2, half, width), jnp.bfloat16),
+            pltpu.VMEM((book.shape[1], groups, LANES), jnp.float32),
             dma((part_dev,)),
             dma((2 * part_dev,)),
             dma((part_dev,)),
@@ -224,9 +233,9 @@
             dma((n_dev,)),
             dma,
         ],
-        compiler_params=pltpu.CompilerParams(collective_id=0, has_side_effects=True, vmem_limit_bytes=56 << 20),
+        compiler_params=pltpu.CompilerParams(collective_id=0, has_side_effects=True, vmem_limit_bytes=22 << 20),
         name="fetch",
-    )(queries, probes, table, codes)
+    )(queries, probes, book, codes)
 
 
 def sort_block(s_ref, x_ref, b, h):
@@ -317,21 +326,36 @@
             x_ref[b0, k * 32 + i] = x[i]
 
 
-def score_kernel(n_cap, sizes_ref, q_ref, own_ref, peer_ref, out_ref, s_ref, x_ref, z_ref):
+def score_kernel(
+    n_cap, idx_ref, sizes_ref, q_ref, own_ref, peer_ref, out_ref,
+    s_ref, x_ref, z_ref, best_ref, back_ref, l_ref, send_sem, recv_sem, local_sem,
+):
     p = pl.program_id(0)
     half = own_ref.shape[2]
     part_dev = pl.num_programs(0)
-
     all_rows = q_ref.shape[0]
+    chip_slots = part_dev * n_cap
+    n_dev = all_rows // chip_slots
+    rep = lax.axis_index("rep")
+    me = lax.axis_index("dom") * lax.axis_size("sub") + lax.axis_index("sub")
+    barrier = pltpu.get_barrier_semaphore()
+
+    @pl.when(p == 0)
+    def _():
+        @pl.loop(1, n_dev)
+        def _(k):
+            pl.semaphore_signal(barrier, inc=1, device_id=device_of((me + k) % n_dev), device_id_type=MESH)
+
     m = lax.broadcasted_iota(jnp.int32, (256, all_rows), 0)
     src = (m // 128) * 32 + m % 32
-    want = src * (part_dev * n_cap) + p * n_cap + (m % 128) // 32
+    want = src * chip_slots + p * n_cap + (m % 128) // 32
     pick = jnp.where(lax.broadcasted_iota(jnp.int32, (256, all_rows), 1) == want, 1.0, 0.0).astype(jnp.bfloat16)
     mine = jnp.dot(pick, q_ref[...], preferred_element_type=jnp.float32).astype(jnp.bfloat16)
 
     for which, ref in enumerate((own_ref, peer_ref)):
         sc = lax.dot_general(ref[0, 0], mine, (((1,), (1,)), ((), ())), preferred_element_type=jnp.float32)
-        ok = lax.broadcasted_iota(jnp.int32, (half, LANES), 0) < sizes_ref[which, p]
+        first = half * (rep if which == 0 else 1 - rep)
+        ok = lax.broadcasted_iota(jnp.int32, (half, LANES), 0) + first < sizes_ref[p]
         for h in range(2):
             blk = jnp.where(ok, sc[:, h * LANES : (h + 1) * LANES], MASKED)
             s_ref[h, pl.ds(which * half // SUBL, half // SUBL)] = blk.reshape(half // SUBL, SUBL, LANES)
@@ -351,41 +375,45 @@
             u = 4 * (blk & 1) + (blk & 2) + (blk >> 2)
             got = z_ref[pl.ds(u, RANKS, stride=SUBL), :].T
             for r in range(n_cap):
-                base = (blk & 1) * 32 * 16 + (blk >> 1) * n_cap + r
-                out_ref[pl.ds(base, 32, stride=16), :] = got[r * 32 : (r + 1) * 32, :]
-
-
-def score(sizes, rows, decoded, n_cap):
-    _, part_dev, half, width = decoded.shape
-    n_rows = rows.shape[0]
-    return pl.pallas_call(
-        functools.partial(score_kernel, n_cap),
-        grid=(part_dev,),
-        out_shape=jax.ShapeDtypeStruct((n_rows, RANKS), jnp.float32),
-        in_specs=[
-            pl.BlockSpec(memory_space=pltpu.SMEM),
-            pl.BlockSpec(memory_space=pltpu.VMEM),
-            pl.BlockSpec((1, 1, half, width), lambda p: (0, p, 0, 0)),
-            pl.BlockSpec((1, 1, half, width), lambda p: (1, p, 0, 0)),
-        ],
-        out_specs=pl.BlockSpec(memory_space=pltpu.VMEM),
-        scratch_shapes=[
-            pltpu.VMEM((2, 2 * half // SUBL, SUBL, LANES), jnp.float32),
-            pltpu.VMEM((8, RANKS, SUBL, LANES), jnp.float32),
-            pltpu.VMEM((RANKS * SUBL, LANES), jnp.float32),
-        ],
-        compiler_params=pltpu.CompilerParams(vmem_limit_bytes=46 << 20),
-        name="score",
-    )(sizes, rows, decoded, decoded)
-
-
-def merge_kernel(idx_ref, r_ref, out_ref, l_ref):
-    rows = out_ref.shape[0]
-    total = l_ref.shape[0]
-
-    @pl.loop(0, total, unroll=8)
-    def _(i):
-        l_ref[pl.ds(i, 1), :] = r_ref[pl.ds(idx_ref[i], 1), :]
+                base = (blk & 1) * 32 * chip_slots + (blk >> 1) * n_cap + r
+                best_ref[pl.ds(base, 32, stride=chip_slots), :] = got[r * 32 : (r + 1) * 32, :]
+
+        def copy(k):
+            t = (me + k) % n_dev
+            return pltpu.make_async_remote_copy(
+                src_ref=best_ref.at[pl.ds(pl.multiple_of(t * chip_slots, chip_slots), chip_slots)],
+                dst_ref=back_ref.at[pl.ds(pl.multiple_of(me * chip_slots, chip_slots), chip_slots)],
+                send_sem=send_sem.at[k],
+                recv_sem=recv_sem.at[k],
+                device_id=device_of(t),
+                device_id_type=MESH,
+            )
+
+        pl.semaphore_wait(barrier, n_dev - 1)
+
+        @pl.loop(1, n_dev)
+        def _(k):
+            copy(k).start()
+
+        mine_rows = pl.ds(pl.multiple_of(me * chip_slots, chip_slots), chip_slots)
+        keep = pltpu.make_async_copy(best_ref.at[mine_rows], back_ref.at[mine_rows], local_sem)
+        keep.start()
+        keep.wait()
+
+        @pl.loop(1, n_dev)
+        def _(k):
+            copy(k).wait()
+
+        final_merge(idx_ref, back_ref, l_ref, out_ref)
+
+
+def final_merge(idx_ref, back_ref, l_ref, out_ref):
+    n_probe, rows = idx_ref.shape
+    for k in range(n_probe):
+
+        @pl.loop(0, rows, unroll=8)
+        def _(i):
+            l_ref[pl.ds(k * rows + i, 1), :] = back_ref[pl.ds(idx_ref[k, i], 1), :]
 
     lists = l_ref[...]
     while lists.shape[0] > rows:
@@ -401,36 +429,48 @@
     out_ref[...] = lists[:, : out_ref.shape[1]]
 
 
-def merge(idx, returned, n_rows):
-    total = idx.shape[0]
+def score(idx, sizes, rows, decoded, n_cap):
+    _, part_dev, half, width = decoded.shape
+    n_rows = rows.shape[0]
+    n_probe, own_rows = idx.shape
+    n_dev = n_rows // (part_dev * n_cap)
     return pl.pallas_call(
-        merge_kernel,
-        out_shape=jax.ShapeDtypeStruct((n_rows, TOPK), jnp.float32),
-        in_specs=[pl.BlockSpec(memory_space=pltpu.SMEM), pl.BlockSpec(memory_space=pltpu.VMEM)],
+        functools.partial(score_kernel, n_cap),
+        grid=(part_dev,),
+        out_shape=jax.ShapeDtypeStruct((own_rows, TOPK), jnp.float32),
+        in_specs=[
+            pl.BlockSpec(memory_space=pltpu.SMEM),
+            pl.BlockSpec(memory_space=pltpu.SMEM),
+            pl.BlockSpec(memory_space=pltpu.VMEM),
+            pl.BlockSpec((1, 1, half, width), lambda p: (0, p, 0, 0)),
+            pl.BlockSpec((1, 1, half, width), lambda p: (1, p, 0, 0)),
+        ],
         out_specs=pl.BlockSpec(memory_space=pltpu.VMEM),
-        scratch_shapes=[pltpu.VMEM((total, RANKS), jnp.float32)],
-        compiler_params=pltpu.CompilerParams(vmem_limit_bytes=16 << 20),
-        name="merge",
-    )(idx, returned)
+        scratch_shapes=[
+            pltpu.VMEM((2, 2 * half // SUBL, SUBL, LANES), jnp.float32),
+            pltpu.VMEM((8, RANKS, SUBL, LANES), jnp.float32),
+            pltpu.VMEM((RANKS * SUBL, LANES), jnp.float32),
+            pltpu.VMEM((n_rows, RANKS), jnp.float32),
+            pltpu.VMEM((n_rows, RANKS), jnp.float32),
+            pltpu.VMEM((n_probe * own_rows, RANKS), jnp.float32),
+            pltpu.SemaphoreType.DMA((n_dev,)),
+            pltpu.SemaphoreType.DMA((n_dev,)),
+            pltpu.SemaphoreType.DMA,
+        ],
+        compiler_params=pltpu.CompilerParams(collective_id=1, has_side_effects=True, vmem_limit_bytes=32 << 20),
+        name="score",
+    )(idx, sizes, rows, decoded, decoded)
 
 
 def local(queries, codebook, probes, codes, part_sizes):
     n_dev = lax.axis_size("dom") * lax.axis_size("sub")
-    rep = lax.axis_index("rep")
     own_rows, width = queries.shape
     n_probe = probes.shape[1]
-    part_dev, n_groups, half = codes.shape
-    n_cent = codebook.shape[1]
+    part_dev = codes.shape[0]
     n_parts = part_dev * n_dev
     n_cap = max(2, 2 * own_rows * n_probe // n_parts)
-    table = jnp.pad(codebook.astype(jnp.float32).transpose(2, 0, 1), ((0, 0), (0, 0), (0, LANES - n_cent)))
-    sizes = jnp.stack([part_sizes - rep * half, part_sizes - (1 - rep) * half])
-    arrived, idx, decoded = fetch(queries, probes, table, codes, n_dev, n_cap)
-    best = score(sizes, arrived.reshape(n_parts * n_cap, width), decoded, n_cap)
-    returned = lax.all_to_all(
-        best.reshape(n_dev, part_dev * n_cap, RANKS), ("dom", "sub"), split_axis=0, concat_axis=0, tiled=True
-    ).reshape(n_parts * n_cap, RANKS)
-    return merge(idx.T.reshape(-1), returned, own_rows)
+    arrived, idx, decoded = fetch(queries, probes.T, codebook.transpose(1, 2, 0), codes, n_dev, n_cap)
+    return score(idx, part_sizes, arrived.reshape(n_parts * n_cap, width), decoded, n_cap)
 
 
 def solution(mesh):

time: 88.2 us -> 75.3 us (0.85)
  waiting for transfers between devices: 12 us -> 0 us
  starting transfers between devices: 8.32 us -> 0 us
  Pallas kernels: 62.2 us -> 70.1 us
  other arithmetic: 1.45 us -> 0 us
  local copies, waits for them, and re-layouts: 3.85 us -> 4.86 us
    pallas_call x1, Pallas kernels: 24 us -> 36.8 us  [score(): pl.pallas_call(functools.partial(score_kernel, n_cap), grid=(part_dev,),...]
    all_to_all x1 -> x0, waiting for transfers between devices: 12 us -> none  [local(): lax.all_to_all(best.reshape(n_dev, part_dev * n_cap, RANKS), ('dom', 'sub...]
    all_to_all x1 -> x0, starting transfers between devices: 8.32 us -> none  [local(): lax.all_to_all(best.reshape(n_dev, part_dev * n_cap, RANKS), ('dom', 'sub...]
    pallas_call x1 -> x0, Pallas kernels: 3.58 us -> none  [merge(): pl.pallas_call(merge_kernel, out_shape=jax.ShapeDtypeStruct((n_rows, TOPK...]
    pallas_call x1, Pallas kernels: 34.6 us -> 33.4 us  [fetch(): pl.pallas_call(functools.partial(fetch_kernel, n_cap), out_shape=(jax.Sha...]
    unnamed x6 -> x11, local copies, waits for them, and re-layouts: 3.71 us -> 4.86 us
  transfers between devices with their start and end apart: 1 -> 0, of which waited for: 1 -> 0; matrix products, arithmetic and copies ran while one was open for 0% -> 0% of each run, Pallas kernels for 0% -> 0%
where the time goes in v4:
time: 75.3 us; the launch traced here: 75 us
  Pallas kernels  70.1 us (93%)
  local copies, waits for them, and re-layouts  4.86 us (6%)
    pallas_call x1, Pallas kernels, score(): pl.pallas_call(functools.partial(score_kernel, n_cap), grid=(part_dev,),...  36.8 us
    pallas_call x1, Pallas kernels, fetch(): pl.pallas_call(functools.partial(fetch_kernel, n_cap), out_shape=(jax.Sha...  33.4 us
    unnamed x11, local copies, waits for them, and re-layouts  4.86 us

profile of v4, /device:TPU:0, one launch (start us, length us, event | category | flops | bytes accessed | tf_op | source)
XLA Modules:
  0.0 75.0 jit_solution(1955853145995308774)
XLA Ops:
  0.0 0.0 copy-start.4
  0.0 0.0 copy-start
  0.0 1.9 %copy-done = s32[4,192,1024]{2,1,0:T(8,128)S(1)} copy-done((s32[4,192,1024]{2,1,0:T(8,128)S(1)}, s32[4,192,1024]{2,1,0:T(8,128)}, u32[]{:S(2)}) %copy-start) | copy-done | bytes 3145752
  1.9 0.0 copy-start.1
  1.9 0.9 %copy-done.1 = bf16[64,768]{1,0:T(8,128)(2,1)S(1)} copy-done((bf16[64,768]{1,0:T(8,128)(2,1)S(1)}, bf16[64,768]{1,0:T(8,128)(2,1)}, u32[]{:S(2)}) %copy-start.1) | copy-done | bytes 98328
  2.8 0.0 copy-start.2
  2.8 0.8 %copy-done.2 = bf16[192,16,4]{0,2,1:T(4,128)(2,1)S(1)} copy-done((bf16[192,16,4]{0,2,1:T(4,128)(2,1)S(1)}, bf16[192,16,4]{0,2,1:T(4,128)(2,1)}, u32[]{:S(2)}) %copy-start.2) | copy-done | bytes 24600
  3.6 0.0 copy-start.3
  3.6 0.7 copy-done.3
  4.2 33.4 %fetch.1 = (bf16[64,16,768]{2,1,0:T(8,128)(2,1)S(1)}, s32[8,64]{1,0:T(8,128)S(1)}, bf16[2,4,1024,768]{3,2,1,0:T(8,128)(2,1)S(1)}) custom-call(bf16[64,768]{1,0:T(8,128)(2,1)S(1)} %copy-done.1, s32[8,64]{1,0:T(8,128)S(1)} %bitcast.5, bf16[16,4,192]{2,1,0:T(4,128)(2,1)S(1)} %bitcast.4, s32[4,192,1024]{2,1,0:T(8,128)S(1)} %copy-done), custom_call_target="tpu_custom_call" | custom-call | tf_op jit(solution)/shard_map/fetch/pallas_call | solution.py:212
  37.6 0.0 copy-done.4
  37.6 36.8 %score.1 = f32[64,100]{1,0:T(8,128)S(1)} custom-call(s32[8,64]{1,0:T(8,128)S(1)} %get-tuple-element.8.idx_ref, s32[4]{0:T(128)S(1)} %copy-done.4, bf16[1024,768]{1,0:T(8,128)(2,1)S(1)} %bitcast.3, bf16[2,4,1024,768]{3,2,1,0:T(8,128)(2,1)S(1)} %get-tuple-element.10.own_ref.peer_ref, bf16[2,4,1024,768]{3,2,1,0:T(8,128)(2,1)S(1)} %get-tuple-element.10.own_ref.peer_ref), custom_call_target="tpu_custom_call" | custom-call | tf_op jit(solution)/shard_map/score/pallas_call | solution.py:437
  74.4 0.6 copy.7
Async XLA Ops:
  0.0 37.6 %copy-start.4 = (s32[4]{0:T(128)S(1)}, s32[4]{0:T(128)}, u32[]{:S(2)}) copy-start(s32[4]{0:T(128)} %sizes_ref.1) | copy-start | bytes 52
  0.0 1.9 %copy-start = (s32[4,192,1024]{2,1,0:T(8,128)S(1)}, s32[4,192,1024]{2,1,0:T(8,128)}, u32[]{:S(2)}) copy-start(s32[4,192,1024]{2,1,0:T(8,128)} %codes_ref.1) | copy-start | bytes 9437188
  1.9 0.9 %copy-start.1 = (bf16[64,768]{1,0:T(8,128)(2,1)S(1)}, bf16[64,768]{1,0:T(8,128)(2,1)}, u32[]{:S(2)}) copy-start(bf16[64,768]{1,0:T(8,128)(2,1)} %q_ref.1) | copy-start | bytes 294916
  2.8 0.8 %copy-start.2 = (bf16[192,16,4]{0,2,1:T(4,128)(2,1)S(1)}, bf16[192,16,4]{0,2,1:T(4,128)(2,1)}, u32[]{:S(2)}) copy-start(bf16[192,16,4]{0,2,1:T(4,128)(2,1)} %param.6) | copy-start | bytes 73732
  3.6 0.7 copy-start.3

commit v5 on v4

--- a/solution.py
+++ b/solution.py
@@ -125,15 +125,21 @@
 
 
 def fetch_kernel(
-    n_cap, q_ref, probes_ref, book_ref, codes_ref, rows_ref, idx_ref, d_out,
-    send_ref, own_ref, peer_ref, t_ref, d_ref, table_ref,
-    in_sem, out_sem, code_send, code_recv, row_send, row_recv, local_sem,
+    n_cap, q_in, probes_in, book_in, codes_ref, rows_ref, idx_ref, d_out,
+    q_ref, probes_ref, book_ref, send_ref, own_ref, peer_ref, t_ref, d_ref, table_ref,
+    small_sem, in_sem, out_sem, code_send, code_recv, row_send, row_recv, local_sem,
 ):
     n_dev = send_ref.shape[0]
     part_dev = codes_ref.shape[0]
     me = lax.axis_index("dom") * lax.axis_size("sub") + lax.axis_index("sub")
     other = {"rep": 1 - lax.axis_index("rep")}
 
+    smalls = [
+        pltpu.make_async_copy(src, dst, small_sem.at[i])
+        for i, (src, dst) in enumerate(((q_in, q_ref), (probes_in, probes_ref), (book_in, book_ref)))
+    ]
+    for c in smalls:
+        c.start()
     loads = [pltpu.make_async_copy(codes_ref.at[p], own_ref.at[p], in_sem.at[p]) for p in range(part_dev)]
     for c in loads:
         c.start()
@@ -144,6 +150,8 @@
     def _(k):
         pl.semaphore_signal(barrier, inc=1, device_id=device_of((me + k) % n_dev), device_id_type=MESH)
 
+    smalls[0].wait()
+    smalls[1].wait()
     route(n_cap, q_ref, probes_ref, send_ref, idx_ref)
     pl.semaphore_wait(barrier, n_dev)
 
@@ -177,6 +185,7 @@
         c.start()
     keep = pltpu.make_async_copy(send_ref.at[me], rows_ref.at[me], local_sem)
     keep.start()
+    smalls[2].wait()
     fill_table(book_ref, table_ref)
 
     writes = []
@@ -216,15 +225,19 @@
             jax.ShapeDtypeStruct(probes.shape, jnp.int32),
             jax.ShapeDtypeStruct((2, part_dev, half, width), jnp.bfloat16),
         ),
-        in_specs=[vmem, vmem, vmem, pl.BlockSpec(memory_space=pltpu.HBM)],
+        in_specs=[pl.BlockSpec(memory_space=pltpu.HBM)] * 4,
         out_specs=[hbm, vmem, hbm],
         scratch_shapes=[
+            pltpu.VMEM(queries.shape, jnp.bfloat16),
+            pltpu.VMEM(probes.shape, jnp.int32),
+            pltpu.VMEM(book.shape, jnp.bfloat16),
             pltpu.VMEM((n_dev, part_dev * n_cap, width), jnp.bfloat16),
             pltpu.VMEM(codes.shape, jnp.int32),
             pltpu.VMEM(codes.shape, jnp.int32),
             pltpu.VMEM((width, half), jnp.bfloat16),
             pltpu.VMEM((2, half, width), jnp.bfloat16),
             pltpu.VMEM((book.shape[1], groups, LANES), jnp.float32),
+            dma((3,)),
             dma((part_dev,)),
             dma((2 * part_dev,)),
             dma((part_dev,)),
@@ -238,97 +251,78 @@
     )(queries, probes, book, codes)
 
 
-def sort_block(s_ref, x_ref, b, h):
-    groups = s_ref.shape[1] // 32
-
-    @pl.loop(0, groups)
+def sort_block(s_ref, x_ref, b, dst):
+    @pl.loop(0, 8)
     def _(g):
         x = exchange([s_ref[b, g * 32 + i] for i in range(32)], SORT32)
         for i in range(32):
             s_ref[b, g * 32 + i] = x[i]
 
-    @pl.loop(0, groups // 2)
+    @pl.loop(0, 4)
     def _(g):
         base = g * 64
-        low = []
-        high = []
-        for i in range(32):
-            u, v = s_ref[b, base + i], s_ref[b, base + 63 - i]
-            high.append(jnp.maximum(u, v))
-            low.append(jnp.minimum(u, v))
-        clean(high)
-        clean(low)
+        high = clean([jnp.maximum(s_ref[b, base + i], s_ref[b, base + 63 - i]) for i in range(32)])
+        low = clean([jnp.minimum(s_ref[b, base + i], s_ref[b, base + 63 - i]) for i in range(32)])
         for i in range(32):
             s_ref[b, base + i] = high[i]
             s_ref[b, base + 32 + i] = low[i]
 
-    @pl.loop(0, groups // 4)
+    @pl.loop(0, 2)
     def _(g):
         base = g * 128
-
-        @pl.loop(0, 32, unroll=8)
-        def _(i):
+        for i in range(32):
             u0, u1 = s_ref[b, base + i], s_ref[b, base + 32 + i]
             v0, v1 = s_ref[b, base + 127 - i], s_ref[b, base + 95 - i]
             h0, h1 = jnp.maximum(u0, v0), jnp.maximum(u1, v1)
             l0, l1 = jnp.minimum(u0, v0), jnp.minimum(u1, v1)
-            x_ref[h, i] = jnp.maximum(h0, h1)
-            x_ref[h, 32 + i] = jnp.minimum(h0, h1)
-            x_ref[h, 64 + i] = jnp.maximum(l0, l1)
-            x_ref[h, 96 + i] = jnp.minimum(l0, l1)
-
-        @pl.loop(0, 4)
+            x_ref[dst, i] = jnp.maximum(h0, h1)
+            x_ref[dst, 32 + i] = jnp.minimum(h0, h1)
+            x_ref[dst, 64 + i] = jnp.maximum(l0, l1)
+            x_ref[dst, 96 + i] = jnp.minimum(l0, l1)
+
+        @pl.loop(0, 4, unroll=2)
         def _(k):
-            x = clean([x_ref[h, k * 32 + i] for i in range(32)])
+            x = clean([x_ref[dst, k * 32 + i] for i in range(32)])
             for i in range(32):
                 s_ref[b, base + k * 32 + i] = x[i]
 
-    @pl.loop(0, 32, unroll=8)
-    def _(i):
-        t = [jnp.maximum(s_ref[b, i + 32 * k], s_ref[b, 255 - i - 32 * k]) for k in range(4)]
-        clean(t)
+    for i in range(32):
+        t = clean([jnp.maximum(s_ref[b, i + 32 * k], s_ref[b, 255 - i - 32 * k]) for k in range(4)])
         for k in range(4):
-            x_ref[h, i + 32 * k] = t[k]
-
-    @pl.loop(0, 4)
+            x_ref[dst, i + 32 * k] = t[k]
+
+    @pl.loop(0, 4, unroll=2)
     def _(k):
-        x = clean([x_ref[h, k * 32 + i] for i in range(32)])
+        x = clean([x_ref[dst, k * 32 + i] for i in range(32)])
         for i in range(32):
-            x_ref[h, k * 32 + i] = x[i]
-
-
-def merge_pair(x_ref, b0, b1, level):
+            x_ref[dst, k * 32 + i] = x[i]
+
+
+def merge_pair(x_ref, y_ref, b0, b1, dst, level):
     bit = 1 << level
-    lower = (lax.broadcasted_iota(jnp.int32, (SUBL, LANES), 0) & bit) == 0
-
-    def joined(i, m):
-        first = jnp.where(lower, x_ref[b0, i], x_ref[b1, i])
-        second = jnp.where(lower, pltpu.roll(x_ref[b0, m], SUBL - bit, 0), pltpu.roll(x_ref[b1, m], bit, 0))
-        return jnp.maximum(first, second)
-
-    @pl.loop(0, 64, unroll=4)
-    def _(i):
-        m = 127 - i
-        s, t = joined(i, m), joined(m, i)
-        x_ref[b0, i] = s
-        x_ref[b0, m] = t
-
-    @pl.loop(0, 32, unroll=8)
-    def _(i):
-        t = clean([x_ref[b0, i + 32 * k] for k in range(4)])
-        for k in range(4):
-            x_ref[b0, i + 32 * k] = t[k]
-
-    @pl.loop(0, 4)
+    sublane = lax.broadcasted_iota(jnp.int32, (SUBL, LANES), 0)
+    lower = (sublane & bit) == 0
+    for i in range(16):
+        first, second = {}, {}
+        for j in [i + 32 * k for k in range(4)] + [31 - i + 32 * k for k in range(4)]:
+            p, q = x_ref[b0, j], x_ref[b1, j]
+            first[j] = jnp.where(lower, p, q)
+            second[j] = jnp.take_along_axis(jnp.where(lower, q, p), sublane ^ bit, axis=0)
+        for r in (i, 31 - i):
+            t = clean([jnp.maximum(first[r + 32 * k], second[127 - r - 32 * k]) for k in range(4)])
+            for k in range(4):
+                y_ref[r + 32 * k] = t[k]
+
+    @pl.loop(0, 4, unroll=2)
     def _(k):
-        x = clean([x_ref[b0, k * 32 + i] for i in range(32)])
+        x = clean([y_ref[k * 32 + i] for i in range(32)])
         for i in range(32):
-            x_ref[b0, k * 32 + i] = x[i]
+            x_ref[dst, k * 32 + i] = x[i]
 
 
 def score_kernel(
     n_cap, idx_ref, sizes_ref, q_ref, own_ref, peer_ref, out_ref,
-    s_ref, x_ref, z_ref, best_ref, back_ref, l_ref, send_sem, recv_sem, local_sem,
+    s_ref, x_ref, y_ref, z_ref, best_ref, back_ref, l_ref, send_sem, recv_sem, local_sem,
 ):
     p = pl.program_id(0)
     half = own_ref.shape[2]
@@ -360,16 +354,21 @@
             blk = jnp.where(ok, sc[:, h * LANES : (h + 1) * LANES], MASKED)
             s_ref[h, pl.ds(which * half // SUBL, half // SUBL)] = blk.reshape(half // SUBL, SUBL, LANES)
 
-    for h in range(2):
+    @pl.loop(0, 2)
+    def _(h):
         sort_block(s_ref, x_ref, h, p * 2 + h)
 
     @pl.when(p == part_dev - 1)
     def _():
-        for b in range(0, 8, 2):
-            merge_pair(x_ref, b, b + 1, 2)
-        for b in range(0, 8, 4):
-            merge_pair(x_ref, b, b + 2, 1)
-        merge_pair(x_ref, 0, 4, 0)
+        @pl.loop(0, 4)
+        def _(b):
+            merge_pair(x_ref, y_ref, 2 * b, 2 * b + 1, b, 2)
+
+        @pl.loop(0, 2)
+        def _(b):
+            merge_pair(x_ref, y_ref, 2 * b, 2 * b + 1, b, 1)
+
+        merge_pair(x_ref, y_ref, 0, 1, 0, 0)
         z_ref[...] = x_ref[0].reshape(RANKS * SUBL, LANES)
         for blk in range(8):
             u = 4 * (blk & 1) + (blk & 2) + (blk >> 2)
@@ -449,6 +448,7 @@
         scratch_shapes=[
             pltpu.VMEM((2, 2 * half // SUBL, SUBL, LANES), jnp.float32),
             pltpu.VMEM((8, RANKS, SUBL, LANES), jnp.float32),
+            pltpu.VMEM((RANKS, SUBL, LANES), jnp.float32),
             pltpu.VMEM((RANKS * SUBL, LANES), jnp.float32),
             pltpu.VMEM((n_rows, RANKS), jnp.float32),
             pltpu.VMEM((n_rows, RANKS), jnp.float32),
@@ -469,7 +469,9 @@
     part_dev = codes.shape[0]
     n_parts = part_dev * n_dev
     n_cap = max(2, 2 * own_rows * n_probe // n_parts)
-    arrived, idx, decoded = fetch(queries, probes.T, codebook.transpose(1, 2, 0), codes, n_dev, n_cap)
+    args = (queries, probes.T, codebook.transpose(1, 2, 0), codes)
+    args = [pltpu.with_memory_space_constraint(x, pltpu.HBM) for x in args]
+    arrived, idx, decoded = fetch(*args, n_dev, n_cap)
     return score(idx, part_sizes, arrived.reshape(n_parts * n_cap, width), decoded, n_cap)
 
 

time: 75.3 us -> 67.4 us (0.90)
  local copies, waits for them, and re-layouts: 4.86 us -> 0.62 us
  Pallas kernels: 70.1 us -> 66.3 us
    unnamed x11 -> x3, local copies, waits for them, and re-layouts: 4.86 us -> 0.62 us
    pallas_call x1, Pallas kernels: 36.8 us -> 33.2 us  [score(): pl.pallas_call(functools.partial(score_kernel, n_cap), grid=(part_dev,),...]
where the time goes in v5:
time: 67.4 us; the launch traced here: 66.9 us
  Pallas kernels  66.3 us (98%)
    pallas_call x1, Pallas kernels, score(): pl.pallas_call(functools.partial(score_kernel, n_cap), grid=(part_dev,),...  33.2 us
    pallas_call x1, Pallas kernels, fetch(): pl.pallas_call(functools.partial(fetch_kernel, n_cap), out_shape=(jax.Sha...  33.1 us

profile of v5, /device:TPU:0, one launch (start us, length us, event | category | flops | bytes accessed | tf_op | source)
XLA Modules:
  0.0 66.9 jit_solution(16750311624291430794)
XLA Ops:
  0.0 0.0 copy-start
  0.0 33.1 %fetch.1 = (bf16[64,16,768]{2,1,0:T(8,128)(2,1)S(1)}, s32[8,64]{1,0:T(8,128)S(1)}, bf16[2,4,1024,768]{3,2,1,0:T(8,128)(2,1)S(1)}) custom-call(bf16[64,768]{1,0:T(8,128)(2,1)} %q_in.1, s32[8,64]{1,0:T(8,128)} %bitcast.5, bf16[16,4,192]{2,1,0:T(4,128)(2,1)} %bitcast.4, s32[4,192,1024]{2,1,0:T(8,128)} %codes_ref.1), custom_call_target="tpu_custom_call" | custom-call | tf_op jit(solution)/shard_map/fetch/pallas_call | solution.py:221
  33.1 0.0 copy-done
  33.1 33.2 %score.1 = f32[64,100]{1,0:T(8,128)S(1)} custom-call(s32[8,64]{1,0:T(8,128)S(1)} %get-tuple-element.8.idx_ref, s32[4]{0:T(128)S(1)} %copy-done, bf16[1024,768]{1,0:T(8,128)(2,1)S(1)} %bitcast.3, bf16[2,4,1024,768]{3,2,1,0:T(8,128)(2,1)S(1)} %get-tuple-element.10.own_ref.peer_ref, bf16[2,4,1024,768]{3,2,1,0:T(8,128)(2,1)S(1)} %get-tuple-element.10.own_ref.peer_ref), custom_call_target="tpu_custom_call" | custom-call | tf_op jit(solution)/shard_map/score/pallas_call | solution.py:436
  66.3 0.6 copy.7
Async XLA Ops:
  0.0 33.1 %copy-start = (s32[4]{0:T(128)S(1)}, s32[4]{0:T(128)}, u32[]{:S(2)}) copy-start(s32[4]{0:T(128)} %sizes_ref.1) | copy-start | bytes 52

commit v6 on v5

v6 whole, which is shorter than its diff:
```python
import functools

import jax
import jax.numpy as jnp
from jax import lax
from jax.experimental import pallas as pl
from jax.experimental.pallas import tpu as pltpu
from jax.sharding import PartitionSpec as P

TOPK = 100
MASKED = -1e30
RANKS = 128
LANES = 128
SUBL = 8


def batcher(n):
    pairs = []

    def merge(lo, cnt, r):
        step = r * 2
        if step < cnt:
            merge(lo, cnt, step)
            merge(lo + r, cnt, step)
            for i in range(lo + r, lo + cnt - r, step):
                pairs.append((i, i + r))
        else:
            pairs.append((lo, lo + r))

    def sort(lo, cnt):
        if cnt > 1:
            m = cnt // 2
            sort(lo, m)
            sort(lo + m, m)
            merge(lo, cnt, 1)

    sort(0, n)
    return pairs


SORT32 = batcher(32)


def exchange(x, pairs):
    for i, j in pairs:
        a, b = x[i], x[j]
        x[i] = jnp.maximum(a, b)
        x[j] = jnp.minimum(a, b)
    return x


def clean(x):
    d = len(x) // 2
    while d:
        exchange(x, [(i, i + d) for i in range(len(x)) if not i & d])
        d //= 2
    return x


MESH = pl.DeviceIdType.MESH


def route(n_cap, q_ref, probes_ref, send_ref, idx_ref):
    rows, width = q_ref.shape
    chunks, n_dev, chip_slots, _ = send_ref.shape
    chunk_slots = n_dev * chip_slots
    slots = chunks * chunk_slots
    each = chip_slots // n_cap
    n = lax.broadcasted_iota(jnp.int32, (slots, rows), 0)
    chip = (n % chunk_slots) // chip_slots
    part = chip * (chunks * each) + (n // chunk_slots) * each + (n % chip_slots) // n_cap
    rank_of = (n % n_cap).astype(jnp.float32)
    n_probe = probes_ref.shape[0]
    hits = [part == probes_ref[k : k + 1, :] for k in range(n_probe)]
    named = hits[0]
    for k in range(1, n_probe):
        named = named | hits[k]
    before = (
        lax.broadcasted_iota(jnp.int32, (rows, rows), 0) < lax.broadcasted_iota(jnp.int32, (rows, rows), 1)
    ).astype(jnp.float32).astype(jnp.bfloat16)
    rank = jnp.dot(named.astype(jnp.float32).astype(jnp.bfloat16), before, preferred_element_type=jnp.float32)
    chosen = named & (rank == rank_of)
    nf = jnp.where(chosen, n, 0)
    for k in range(n_probe):
        idx_ref[k : k + 1, :] = jnp.sum(jnp.where(hits[k], nf, 0), axis=0, keepdims=True)
    a = lax.broadcasted_iota(jnp.int32, (width, width), 0)
    b = lax.broadcasted_iota(jnp.int32, (width, width), 1)
    groups = width // 4
    j = (b >= groups).astype(jnp.int32) + (b >= 2 * groups).astype(jnp.int32) + (b >= 3 * groups).astype(jnp.int32)
    perm = jnp.where(a == (b - groups * j) * 4 + j, 1.0, 0.0).astype(jnp.bfloat16)
    moved = jnp.dot(q_ref[...], perm, preferred_element_type=jnp.float32).astype(jnp.bfloat16)
    pick = jnp.where(chosen, 1.0, 0.0).astype(jnp.bfloat16)
    picked = jnp.dot(pick, moved, preferred_element_type=jnp.float32)
    send_ref[...] = picked.astype(jnp.bfloat16).reshape(send_ref.shape)


def fill_table(book_ref, table_ref):
    n_cent, n_feat, groups = book_ref.shape
    for j in range(n_feat):
        plane = book_ref[:, j, :].astype(jnp.float32)
        wide = jnp.concatenate([plane, jnp.zeros((LANES - n_cent, groups), jnp.float32)], axis=0)
        table_ref[j] = wide.T


def decode(table_ref, codes_ref, p, t_ref, d_ref):
    groups, half = codes_ref.shape[1:]

    @pl.loop(0, groups // 16)
    def _(g):
        rows = pl.ds(pl.multiple_of(g * 16, 16), 16)
        tab = [table_ref[j, rows, :] for j in range(4)]
        for t in range(half // LANES):
            cols = slice(t * LANES, (t + 1) * LANES)
            c = codes_ref[p, rows, cols]
            for j in range(4):
                val = jnp.take_along_axis(tab[j], c, axis=1)
                t_ref[pl.ds(pl.multiple_of(j * groups + g * 16, 16), 16), cols] = val.astype(jnp.bfloat16)

    @pl.loop(0, half // 256)
    def _(t):
        cols = pl.ds(pl.multiple_of(t * 256, 256), 256)
        d_ref[p, cols, :] = t_ref[:, cols].T


def sort_block(s_ref, x_ref, b, dst):
    @pl.loop(0, 8)
    def _(g):
        x = exchange([s_ref[b, g * 32 + i] for i in range(32)], SORT32)
        for i in range(32):
            s_ref[b, g * 32 + i] = x[i]

    @pl.loop(0, 4)
    def _(g):
        base = g * 64
        high = clean([jnp.maximum(s_ref[b, base + i], s_ref[b, base + 63 - i]) for i in range(32)])
        low = clean([jnp.minimum(s_ref[b, base + i], s_ref[b, base + 63 - i]) for i in range(32)])
        for i in range(32):
            s_ref[b, base + i] = high[i]
            s_ref[b, base + 32 + i] = low[i]

    @pl.loop(0, 2)
    def _(g):
        base = g * 128
        for i in range(32):
            u0, u1 = s_ref[b, base + i], s_ref[b, base + 32 + i]
            v0, v1 = s_ref[b, base + 127 - i], s_ref[b, base + 95 - i]
            h0, h1 = jnp.maximum(u0, v0), jnp.maximum(u1, v1)
            l0, l1 = jnp.minimum(u0, v0), jnp.minimum(u1, v1)
            x_ref[dst, i] = jnp.maximum(h0, h1)
            x_ref[dst, 32 + i] = jnp.minimum(h0, h1)
            x_ref[dst, 64 + i] = jnp.maximum(l0, l1)
            x_ref[dst, 96 + i] = jnp.minimum(l0, l1)

        @pl.loop(0, 4, unroll=2)
        def _(k):
            x = clean([x_ref[dst, k * 32 + i] for i in range(32)])
            for i in range(32):
                s_ref[b, base + k * 32 + i] = x[i]

    for i in range(32):
        t = clean([jnp.maximum(s_ref[b, i + 32 * k], s_ref[b, 255 - i - 32 * k]) for k in range(4)])
        for k in range(4):
            x_ref[dst, i + 32 * k] = t[k]

    @pl.loop(0, 4, unroll=2)
    def _(k):
        x = clean([x_ref[dst, k * 32 + i] for i in range(32)])
        for i in range(32):
            x_ref[dst, k * 32 + i] = x[i]


def merge_pair(x_ref, y_ref, b0, b1, dst, level):
    bit = 1 << level
    sublane = lax.broadcasted_iota(jnp.int32, (SUBL, LANES), 0)
    lower = (sublane & bit) == 0
    for i in range(16):
        first, second = {}, {}
        for j in [i + 32 * k for k in range(4)] + [31 - i + 32 * k for k in range(4)]:
            p, q = x_ref[b0, j], x_ref[b1, j]
            first[j] = jnp.where(lower, p, q)
            second[j] = jnp.take_along_axis(jnp.where(lower, q, p), sublane ^ bit, axis=0)
        for r in (i, 31 - i):
            t = clean([jnp.maximum(first[r + 32 * k], second[127 - r - 32 * k]) for k in range(4)])
            for k in range(4):
                y_ref[r + 32 * k] = t[k]

    @pl.loop(0, 4, unroll=2)
    def _(k):
        x = clean([y_ref[k * 32 + i] for i in range(32)])
        for i in range(32):
            x_ref[dst, k * 32 + i] = x[i]


def kernel(
    n_cap, sizes_ref, q_in, probes_in, book_in, codes_ref, out_ref,
    q_ref, probes_ref, book_ref, send_ref, rows_ref, own_ref, t_ref, d_own, d_peer, table_ref,
    s_ref, x_ref, y_ref, z_ref, best_ref, back_ref, l_ref, idx_vmem, idx_ref,
    small_sem, in_sem, code_send, code_recv, row_send, row_recv, best_send, best_recv, row_keep, best_keep,
):
    chunks, n_dev, chip_slots, width = send_ref.shape
    part_dev, _, half = codes_ref.shape
    each = part_dev // chunks
    rep = lax.axis_index("rep")
    n_sub, n_dom = lax.axis_size("sub"), lax.axis_size("dom")
    my_dom, my_sub = lax.axis_index("dom"), lax.axis_index("sub")
    me = my_dom * n_sub + my_sub
    other = {"rep": 1 - rep}

    smalls = [
        pltpu.make_async_copy(src, dst, small_sem.at[i])
        for i, (src, dst) in enumerate(((q_in, q_ref), (probes_in, probes_ref), (book_in, book_ref)))
    ]
    for c in smalls:
        c.start()
    loads = [pltpu.make_async_copy(codes_ref.at[p], own_ref.at[p], in_sem.at[p]) for p in range(part_dev)]
    for c in loads:
        c.start()
    barrier = pltpu.get_barrier_semaphore()
    pl.semaphore_signal(barrier, inc=1, device_id=other, device_id_type=MESH)

    def partners(visit):
        for ks in range(1, n_sub):
            visit(my_dom, lax.rem(my_sub + ks, n_sub))

        @pl.loop(1, n_dom)
        def _(kd):
            for ks in range(n_sub):
                visit(lax.rem(my_dom + kd, n_dom), lax.rem(my_sub + ks, n_sub))

    @partners
    def _(td, ts):
        pl.semaphore_signal(barrier, inc=1, device_id={"dom": td, "sub": ts}, device_id_type=MESH)

    for c in smalls:
        c.wait()
    route(n_cap, q_ref, probes_ref, send_ref, idx_vmem)
    fill_table(book_ref, table_ref)
    pl.semaphore_wait(barrier, n_dev)

    def exchange_all(src, dst, send_sem, recv_sem, keep_sem):
        @partners
        def _(td, ts):
            pltpu.make_async_remote_copy(
                src_ref=src.at[td * n_sub + ts],
                dst_ref=dst.at[me],
                send_sem=send_sem,
                recv_sem=recv_sem,
                device_id={"dom": td, "sub": ts},
                device_id_type=MESH,
            ).start()

        pltpu.make_async_copy(src.at[me], dst.at[me], keep_sem).start()

    def finish_recv(src, dst, recv_sem, keep_sem):
        most = pl.ds(0, n_dev - 1)
        pltpu.make_async_copy(src.at[most], dst.at[most], recv_sem).wait()
        pltpu.make_async_copy(src.at[me], dst.at[me], keep_sem).wait()

    def finish_send(src, dst, send_sem):
        most = pl.ds(0, n_dev - 1)
        pltpu.make_async_copy(src.at[most], dst.at[most], send_sem).wait()

    swaps = [
        pltpu.make_async_remote_copy(
            src_ref=d_own.at[p],
            dst_ref=d_peer.at[p],
            send_sem=code_send.at[p],
            recv_sem=code_recv.at[p],
            device_id=other,
            device_id_type=MESH,
        )
        for p in range(part_dev)
    ]
    for c in range(chunks):
        exchange_all(send_ref.at[c], rows_ref.at[c], row_send.at[c], row_recv.at[c], row_keep.at[c])
        for p in range(c * each, (c + 1) * each):
            loads[p].wait()
            decode(table_ref, own_ref, p, t_ref, d_own)
            swaps[p].start()
    for_idx = pltpu.make_async_copy(idx_vmem, idx_ref, small_sem.at[0])
    for_idx.start()

    for c in range(chunks):
        finish_recv(send_ref.at[c], rows_ref.at[c], row_recv.at[c], row_keep.at[c])
        rows = rows_ref[c].reshape(n_dev * chip_slots, width)
        for e in range(each):
            p = c * each + e
            m = lax.broadcasted_iota(jnp.int32, (256, rows.shape[0]), 0)
            want = ((m // 128) * 32 + m % 32) * chip_slots + e * n_cap + (m % 128) // 32
            pick = jnp.where(lax.broadcasted_iota(jnp.int32, m.shape, 1) == want, 1.0, 0.0).astype(jnp.bfloat16)
            mine = jnp.dot(pick, rows, preferred_element_type=jnp.float32).astype(jnp.bfloat16)
            for which, ref in enumerate((d_own, d_peer)):
                if which == 1:
                    swaps[p].wait_recv()
                sc = lax.dot_general(ref[p], mine, (((1,), (1,)), ((), ())), preferred_element_type=jnp.float32)
                first = half * (rep if which == 0 else 1 - rep)
                ok = lax.broadcasted_iota(jnp.int32, (half, LANES), 0) + first < sizes_ref[p]
                for h in range(2):
                    blk = jnp.where(ok, sc[:, h * LANES : (h + 1) * LANES], MASKED)
                    s_ref[h, pl.ds(which * half // SUBL, half // SUBL)] = blk.reshape(half // SUBL, SUBL, LANES)

            @pl.loop(0, 2)
            def _(h):
                sort_block(s_ref, x_ref, h, e * 2 + h)

        @pl.loop(0, 2)
        def _(b):
            merge_pair(x_ref, y_ref, 2 * b, 2 * b + 1, b, 2)

        merge_pair(x_ref, y_ref, 0, 1, 0, 1)
        merge_pair(x_ref, y_ref, 0, 0, 0, 0)
        z_ref[...] = x_ref[0].reshape(RANKS * SUBL, LANES)
        for blk in range(4):
            u = 4 * (blk & 1) + (blk & 2)
            got = z_ref[pl.ds(u, RANKS, stride=SUBL), :].T
            for r in range(n_cap):
                slot = (blk >> 1) * n_cap + r
                best_ref[c, (blk & 1) * 32 : (blk & 1) * 32 + 32, slot, :] = got[r * 32 : (r + 1) * 32, :]
        exchange_all(best_ref.at[c], back_ref.at[c], best_send.at[c], best_recv.at[c], best_keep.at[c])

    for_idx.wait()
    for c in range(chunks):
        finish_recv(best_ref.at[c], back_ref.at[c], best_recv.at[c], best_keep.at[c])
    final_merge(idx_ref, back_ref, l_ref, out_ref)
    for c in range(chunks):
        finish_send(send_ref.at[c], rows_ref.at[c], row_send.at[c])
        finish_send(best_ref.at[c], back_ref.at[c], best_send.at[c])
    for c in swaps:
        c.wait_send()


def final_merge(idx_ref, back_ref, l_ref, out_ref):
    n_probe, rows = idx_ref.shape
    flat = back_ref.reshape(l_ref.shape[0] * 2, RANKS)
    for k in range(n_probe):

        @pl.loop(0, rows, unroll=8)
        def _(i):
            n = idx_ref[k, i]
            l_ref[pl.ds(k * rows + i, 1), :] = flat[pl.ds(n, 1), :]

    lists = l_ref[...]
    while lists.shape[0] > rows:
        h = lists.shape[0] // 2
        lane = lax.broadcasted_iota(jnp.int32, (h, RANKS), 1)
        a, b = lists[:h], lists[h:]
        lists = jnp.maximum(a, jnp.take_along_axis(b, RANKS - 1 - lane, axis=1))
        d = RANKS // 2
        while d:
            other = jnp.take_along_axis(lists, lane ^ d, axis=1)
            lists = jnp.where((lane & d) == 0, jnp.maximum(lists, other), jnp.minimum(lists, other))
            d //= 2
    out_ref[...] = lists[:, : out_ref.shape[1]]


def local(queries, codebook, probes, codes, part_sizes):
    n_dev = lax.axis_size("dom") * lax.axis_size("sub")
    own_rows, width = queries.shape
    n_probe = probes.shape[1]
    part_dev, groups, half = codes.shape
    n_cap = max(2, 2 * own_rows * n_probe // (part_dev * n_dev))
    chunks = 2
    chip_slots = part_dev * n_cap // chunks
    book = codebook.transpose(1, 2, 0)
    args = [pltpu.with_memory_space_constraint(x, pltpu.HBM) for x in (queries, probes.T, book, codes)]
    hbm = pl.BlockSpec(memory_space=pltpu.HBM)
    vmem, dma = pltpu.VMEM, pltpu.SemaphoreType.DMA
    lists = vmem((chunks, n_dev, chip_slots, RANKS), jnp.float32)
    rows = vmem((chunks, n_dev, chip_slots, width), jnp.bfloat16)
    decoded = vmem((part_dev, half, width), jnp.bfloat16)
    return pl.pallas_call(
        functools.partial(kernel, n_cap),
        out_shape=jax.ShapeDtypeStruct((own_rows, TOPK), jnp.float32),
        in_specs=[pl.BlockSpec(memory_space=pltpu.SMEM), hbm, hbm, hbm, hbm],
        out_specs=pl.BlockSpec(memory_space=pltpu.VMEM),
        scratch_shapes=[
            vmem(queries.shape, jnp.bfloat16),
            vmem((n_probe, own_rows), jnp.int32),
            vmem(book.shape, jnp.bfloat16),
            rows,
            rows,
            vmem(codes.shape, jnp.int32),
            vmem((width, half), jnp.bfloat16),
            decoded,
            decoded,
            vmem((book.shape[1], groups, LANES), jnp.float32),
            vmem((2, 2 * half // SUBL, SUBL, LANES), jnp.float32),
            vmem((4, RANKS, SUBL, LANES), jnp.float32),
            vmem((RANKS, SUBL, LANES), jnp.float32),
            vmem((RANKS * SUBL, LANES), jnp.float32),
            lists,
            lists,
            vmem((n_probe * own_rows, RANKS), jnp.float32),
            vmem((n_probe, own_rows), jnp.int32),
            pltpu.SMEM((n_probe, own_rows), jnp.int32),
            dma((3,)),
            dma((part_dev,)),
            dma((part_dev,)),
            dma((part_dev,)),
            dma((chunks,)),
            dma((chunks,)),
            dma((chunks,)),
            dma((chunks,)),
            dma((chunks,)),
            dma((chunks,)),
        ],
        compiler_params=pltpu.CompilerParams(collective_id=0, has_side_effects=True, vmem_limit_bytes=56 << 20),
        name="search",
    )(part_sizes, *args)


def solution(mesh):
    in_specs = (
        P(("dom", "sub", "rep"), None),
        P(),
        P(("dom", "sub", "rep"), None),
        P(("dom", "sub"), None, "rep"),
        P(("dom", "sub")),
    )
    out_specs = P(("dom", "sub", "rep"), None)
    return jax.shard_map(local, mesh=mesh, in_specs=in_specs, out_specs=out_specs, check_vma=False)
```

time: 67.4 us -> 60.3 us (0.89)
  Pallas kernels: 66.3 us -> 58.8 us
  local copies, waits for them, and re-layouts: 0.62 us -> 1.38 us
    pallas_call x2 -> x1, Pallas kernels: 66.3 us -> 58.8 us  [local(): pl.pallas_call(functools.partial(kernel, n_cap), out_shape=jax.ShapeDtype...]
    unnamed x3 -> x1, local copies, waits for them, and re-layouts: 0.62 us -> 1.38 us
where the time goes in v6:
time: 60.3 us; the launch traced here: 60.2 us
  Pallas kernels  58.8 us (98%)
  local copies, waits for them, and re-layouts  1.38 us (2%)
    pallas_call x1, Pallas kernels, local(): pl.pallas_call(functools.partial(kernel, n_cap), out_shape=jax.ShapeDtype...  58.8 us
    unnamed x1, local copies, waits for them, and re-layouts  1.38 us

profile of v6, /device:TPU:0, one launch (start us, length us, event | category | flops | bytes accessed | tf_op | source)
XLA Modules:
  0.0 60.2 jit_solution(10390624268105335379)
XLA Ops:
  0.0 58.8 %search.1 = f32[64,100]{1,0:T(8,128)} custom-call(s32[4]{0:T(128)} %sizes_ref.1, bf16[64,768]{1,0:T(8,128)(2,1)} %q_in.1, s32[8,64]{1,0:T(8,128)} %bitcast.3, bf16[16,4,192]{2,1,0:T(4,128)(2,1)} %bitcast.2, s32[4,192,1024]{2,1,0:T(8,128)} %codes_ref.1), custom_call_target="tpu_custom_call" | custom-call | tf_op jit(solution)/shard_map/search/pallas_call | solution.py:371
  58.8 1.4 %copy.7 = f32[64,100]{1,0:T(8,128)} copy(f32[64,100]{1,0:T(8,128)} %search.1) | data formatting | bytes 51200

commit v7 on v6

--- a/solution.py
+++ b/solution.py
@@ -192,8 +192,8 @@
 
 
 def kernel(
-    n_cap, sizes_ref, q_in, probes_in, book_in, codes_ref, out_ref,
-    q_ref, probes_ref, book_ref, send_ref, rows_ref, own_ref, t_ref, d_own, d_peer, table_ref,
+    n_cap, sizes_in, q_in, probes_in, book_in, codes_ref, out_ref,
+    sizes_ref, q_ref, probes_ref, book_ref, send_ref, rows_ref, own_ref, t_ref, d_own, d_peer, table_ref,
     s_ref, x_ref, y_ref, z_ref, best_ref, back_ref, l_ref, idx_vmem, idx_ref,
     small_sem, in_sem, code_send, code_recv, row_send, row_recv, best_send, best_recv, row_keep, best_keep,
 ):
@@ -208,7 +208,9 @@
 
     smalls = [
         pltpu.make_async_copy(src, dst, small_sem.at[i])
-        for i, (src, dst) in enumerate(((q_in, q_ref), (probes_in, probes_ref), (book_in, book_ref)))
+        for i, (src, dst) in enumerate(
+            ((q_in, q_ref), (probes_in, probes_ref), (book_in, book_ref), (sizes_in, sizes_ref))
+        )
     ]
     for c in smalls:
         c.start()
@@ -271,17 +273,24 @@
         )
         for p in range(part_dev)
     ]
-    for c in range(chunks):
+    def send_rows(c):
         exchange_all(send_ref.at[c], rows_ref.at[c], row_send.at[c], row_recv.at[c], row_keep.at[c])
-        for p in range(c * each, (c + 1) * each):
-            loads[p].wait()
-            decode(table_ref, own_ref, p, t_ref, d_own)
+
+    send_rows(0)
+    for p in range(part_dev):
+        loads[p].wait()
+        decode(table_ref, own_ref, p, t_ref, d_own)
+        if p < each:
             swaps[p].start()
+    send_rows(1)
     for_idx = pltpu.make_async_copy(idx_vmem, idx_ref, small_sem.at[0])
     for_idx.start()
 
     for c in range(chunks):
         finish_recv(send_ref.at[c], rows_ref.at[c], row_recv.at[c], row_keep.at[c])
+        if c == 0:
+            for p in range(each, part_dev):
+                swaps[p].start()
         rows = rows_ref[c].reshape(n_dev * chip_slots, width)
         for e in range(each):
             p = c * each + e
@@ -362,7 +371,7 @@
     chunks = 2
     chip_slots = part_dev * n_cap // chunks
     book = codebook.transpose(1, 2, 0)
-    args = [pltpu.with_memory_space_constraint(x, pltpu.HBM) for x in (queries, probes.T, book, codes)]
+    args = [pltpu.with_memory_space_constraint(x, pltpu.HBM) for x in (part_sizes, queries, probes.T, book, codes)]
     hbm = pl.BlockSpec(memory_space=pltpu.HBM)
     vmem, dma = pltpu.VMEM, pltpu.SemaphoreType.DMA
     lists = vmem((chunks, n_dev, chip_slots, RANKS), jnp.float32)
@@ -371,9 +380,10 @@
     return pl.pallas_call(
         functools.partial(kernel, n_cap),
         out_shape=jax.ShapeDtypeStruct((own_rows, TOPK), jnp.float32),
-        in_specs=[pl.BlockSpec(memory_space=pltpu.SMEM), hbm, hbm, hbm, hbm],
+        in_specs=[hbm] * 5,
         out_specs=pl.BlockSpec(memory_space=pltpu.VMEM),
         scratch_shapes=[
+            pltpu.SMEM(part_sizes.shape, jnp.int32),
             vmem(queries.shape, jnp.bfloat16),
             vmem((n_probe, own_rows), jnp.int32),
             vmem(book.shape, jnp.bfloat16),
@@ -393,7 +403,7 @@
             vmem((n_probe * own_rows, RANKS), jnp.float32),
             vmem((n_probe, own_rows), jnp.int32),
             pltpu.SMEM((n_probe, own_rows), jnp.int32),
-            dma((3,)),
+            dma((4,)),
             dma((part_dev,)),
             dma((part_dev,)),
             dma((part_dev,)),
@@ -404,9 +414,9 @@
             dma((chunks,)),
             dma((chunks,)),
         ],
-        compiler_params=pltpu.CompilerParams(collective_id=0, has_side_effects=True, vmem_limit_bytes=56 << 20),
+        compiler_params=pltpu.CompilerParams(collective_id=0, has_side_effects=True, vmem_limit_bytes=40 << 20),
         name="search",
-    )(part_sizes, *args)
+    )(*args)
 
 
 def solution(mesh):

time: 60.3 us -> 53.2 us (0.88)
  Pallas kernels: 58.8 us -> 52.4 us
  local copies, waits for them, and re-layouts: 1.38 us -> 0.62 us
    pallas_call x1, Pallas kernels: 58.8 us -> 52.4 us  [local(): pl.pallas_call(functools.partial(kernel, n_cap), out_shape=jax.ShapeDtype...]
    unnamed x1, local copies, waits for them, and re-layouts: 1.38 us -> 0.62 us
where the time goes in v7:
time: 53.2 us; the launch traced here: 53.1 us
  Pallas kernels  52.4 us (98%)
  local copies, waits for them, and re-layouts  0.62 us (1%)
    pallas_call x1, Pallas kernels, local(): pl.pallas_call(functools.partial(kernel, n_cap), out_shape=jax.ShapeDtype...  52.4 us

profile of v7, /device:TPU:0, one launch (start us, length us, event | category | flops | bytes accessed | tf_op | source)
XLA Modules:
  0.0 53.1 jit_solution(8525251065010301512)
XLA Ops:
  0.0 52.4 %search.1 = f32[64,100]{1,0:T(8,128)S(1)} custom-call(s32[4]{0:T(128)} %sizes_in.1, bf16[64,768]{1,0:T(8,128)(2,1)} %q_in.1, s32[8,64]{1,0:T(8,128)} %bitcast.3, bf16[16,4,192]{2,1,0:T(4,128)(2,1)} %bitcast.2, s32[4,192,1024]{2,1,0:T(8,128)} %codes_ref.1), custom_call_target="tpu_custom_call" | custom-call | tf_op jit(solution)/shard_map/search/pallas_call | solution.py:380
  52.5 0.6 %copy.7 = f32[64,100]{1,0:T(8,128)} copy(f32[64,100]{1,0:T(8,128)S(1)} %search.1) | data formatting | bytes 51200

commit v8 on v7

--- a/solution.py
+++ b/solution.py
@@ -194,7 +194,7 @@
 def kernel(
     n_cap, sizes_in, q_in, probes_in, book_in, codes_ref, out_ref,
     sizes_ref, q_ref, probes_ref, book_ref, send_ref, rows_ref, own_ref, t_ref, d_own, d_peer, table_ref,
-    s_ref, x_ref, y_ref, z_ref, best_ref, back_ref, l_ref, idx_vmem, idx_ref,
+    s_ref, x_ref, y_ref, z_ref, best_ref, back_ref, idx_ref,
     small_sem, in_sem, code_send, code_recv, row_send, row_recv, best_send, best_recv, row_keep, best_keep,
 ):
     chunks, n_dev, chip_slots, width = send_ref.shape
@@ -235,7 +235,7 @@
 
     for c in smalls:
         c.wait()
-    route(n_cap, q_ref, probes_ref, send_ref, idx_vmem)
+    route(n_cap, q_ref, probes_ref, send_ref, idx_ref)
     fill_table(book_ref, table_ref)
     pl.semaphore_wait(barrier, n_dev)
 
@@ -283,8 +283,6 @@
         if p < each:
             swaps[p].start()
     send_rows(1)
-    for_idx = pltpu.make_async_copy(idx_vmem, idx_ref, small_sem.at[0])
-    for_idx.start()
 
     for c in range(chunks):
         finish_recv(send_ref.at[c], rows_ref.at[c], row_recv.at[c], row_keep.at[c])
@@ -327,10 +325,12 @@
                 best_ref[c, (blk & 1) * 32 : (blk & 1) * 32 + 32, slot, :] = got[r * 32 : (r + 1) * 32, :]
         exchange_all(best_ref.at[c], back_ref.at[c], best_send.at[c], best_recv.at[c], best_keep.at[c])
 
-    for_idx.wait()
+    found = None
     for c in range(chunks):
         finish_recv(best_ref.at[c], back_ref.at[c], best_recv.at[c], best_keep.at[c])
-    final_merge(idx_ref, back_ref, l_ref, out_ref)
+        got = select_lists(idx_ref, back_ref[c].reshape(n_dev * chip_slots, RANKS), c)
+        found = got if found is None else found + got
+    final_merge(found, out_ref)
     for c in range(chunks):
         finish_send(send_ref.at[c], rows_ref.at[c], row_send.at[c])
         finish_send(best_ref.at[c], back_ref.at[c], best_send.at[c])
@@ -338,28 +338,53 @@
         c.wait_send()
 
 
-def final_merge(idx_ref, back_ref, l_ref, out_ref):
-    n_probe, rows = idx_ref.shape
-    flat = back_ref.reshape(l_ref.shape[0] * 2, RANKS)
-    for k in range(n_probe):
-
-        @pl.loop(0, rows, unroll=8)
-        def _(i):
-            n = idx_ref[k, i]
-            l_ref[pl.ds(k * rows + i, 1), :] = flat[pl.ds(n, 1), :]
-
-    lists = l_ref[...]
-    while lists.shape[0] > rows:
-        h = lists.shape[0] // 2
-        lane = lax.broadcasted_iota(jnp.int32, (h, RANKS), 1)
-        a, b = lists[:h], lists[h:]
-        lists = jnp.maximum(a, jnp.take_along_axis(b, RANKS - 1 - lane, axis=1))
-        d = RANKS // 2
+def select_lists(idx_ref, lists, c):
+    n_slots = lists.shape[0]
+    wanted = jnp.concatenate([idx_ref[k : k + 1, :] for k in range(idx_ref.shape[0])], axis=1)
+    slot = lax.broadcasted_iota(jnp.int32, (n_slots, wanted.shape[1]), 0) + c * n_slots
+    pick = jnp.where(slot == wanted, 1.0, 0.0).astype(jnp.bfloat16)
+    rest = lists.T
+    parts = []
+    for _ in range(3):
+        part = rest.astype(jnp.bfloat16)
+        rest = rest - part.astype(jnp.float32)
+        parts.append(part)
+    got = jnp.dot(jnp.concatenate(parts, axis=0), pick, preferred_element_type=jnp.float32)
+    return got[:RANKS] + got[RANKS : 2 * RANKS] + got[2 * RANKS :]
+
+
+def final_merge(x, out_ref):
+    rows, n_out = out_ref.shape
+    sublane = lax.broadcasted_iota(jnp.int32, (SUBL, LANES), 0)
+    n_i = RANKS // SUBL
+    cols = [
+        [x[i * SUBL : (i + 1) * SUBL, t * LANES : (t + 1) * LANES] for i in range(n_i)]
+        for t in range(x.shape[1] // LANES)
+    ]
+
+    def permuted(v, index):
+        return jnp.take_along_axis(v, index, axis=0)
+
+    def joined(a, b):
+        m = clean([jnp.maximum(a[i], permuted(b[n_i - 1 - i], SUBL - 1 - sublane)) for i in range(n_i)])
+        d = SUBL // 2
         while d:
-            other = jnp.take_along_axis(lists, lane ^ d, axis=1)
-            lists = jnp.where((lane & d) == 0, jnp.maximum(lists, other), jnp.minimum(lists, other))
+            near = (sublane & d) == 0
+            for i in range(n_i):
+                other = permuted(m[i], sublane ^ d)
+                m[i] = jnp.where(near, jnp.maximum(m[i], other), jnp.minimum(m[i], other))
             d //= 2
-    out_ref[...] = lists[:, : out_ref.shape[1]]
+        return m
+
+    while len(cols) > 1:
+        h = len(cols) // 2
+        cols = [joined(cols[t], cols[t + h]) for t in range(h)]
+    m = cols[0]
+    width = LANES
+    while width > rows:
+        width //= 2
+        m = joined(m, [pltpu.roll(v, width, 1) for v in m])
+    out_ref[...] = jnp.concatenate(m, axis=0).T[:rows, :n_out]
 
 
 def local(queries, codebook, probes, codes, part_sizes):
@@ -400,9 +425,7 @@
             vmem((RANKS * SUBL, LANES), jnp.float32),
             lists,
             lists,
-            vmem((n_probe * own_rows, RANKS), jnp.float32),
             vmem((n_probe, own_rows), jnp.int32),
-            pltpu.SMEM((n_probe, own_rows), jnp.int32),
             dma((4,)),
             dma((part_dev,)),
             dma((part_dev,)),

time: 53.2 us -> 50.9 us (0.957)
  Pallas kernels: 52.4 us -> 50.2 us
    pallas_call x1, Pallas kernels: 52.4 us -> 50.2 us  [local(): pl.pallas_call(functools.partial(kernel, n_cap), out_shape=jax.ShapeDtype...]
where the time goes in v8:
time: 50.9 us; the launch traced here: 50.8 us
  Pallas kernels  50.2 us (99%)
  local copies, waits for them, and re-layouts  0.62 us (1%)
    pallas_call x1, Pallas kernels, local(): pl.pallas_call(functools.partial(kernel, n_cap), out_shape=jax.ShapeDtype...  50.2 us

profile of v8, /device:TPU:0, one launch (start us, length us, event | category | flops | bytes accessed | tf_op | source)
XLA Modules:
  0.0 50.8 jit_solution(9279744956919862344)
XLA Ops:
  0.0 50.2 %search.1 = f32[64,100]{1,0:T(8,128)S(1)} custom-call(s32[4]{0:T(128)} %sizes_in.1, bf16[64,768]{1,0:T(8,128)(2,1)} %q_in.1, s32[8,64]{1,0:T(8,128)} %bitcast.3, bf16[16,4,192]{2,1,0:T(4,128)(2,1)} %bitcast.2, s32[4,192,1024]{2,1,0:T(8,128)} %codes_ref.1), custom_call_target="tpu_custom_call" | custom-call | tf_op jit(solution)/shard_map/search/pallas_call | solution.py:405
  50.2 0.6 %copy.7 = f32[64,100]{1,0:T(8,128)} copy(f32[64,100]{1,0:T(8,128)S(1)} %search.1) | data formatting | bytes 51200

commit v9 on v8

--- a/solution.py
+++ b/solution.py
@@ -122,51 +122,51 @@
         d_ref[p, cols, :] = t_ref[:, cols].T
 
 
-def sort_block(s_ref, x_ref, b, dst):
-    @pl.loop(0, 8)
-    def _(g):
-        x = exchange([s_ref[b, g * 32 + i] for i in range(32)], SORT32)
-        for i in range(32):
-            s_ref[b, g * 32 + i] = x[i]
-
+def sort_half(s_ref, x_ref, b, start):
     @pl.loop(0, 4)
     def _(g):
-        base = g * 64
+        base = start + g * 32
+        x = exchange([s_ref[b, base + i] for i in range(32)], SORT32)
+        for i in range(32):
+            s_ref[b, base + i] = x[i]
+
+    @pl.loop(0, 2)
+    def _(g):
+        base = start + g * 64
         high = clean([jnp.maximum(s_ref[b, base + i], s_ref[b, base + 63 - i]) for i in range(32)])
         low = clean([jnp.minimum(s_ref[b, base + i], s_ref[b, base + 63 - i]) for i in range(32)])
         for i in range(32):
             s_ref[b, base + i] = high[i]
             s_ref[b, base + 32 + i] = low[i]
 
-    @pl.loop(0, 2)
-    def _(g):
-        base = g * 128
+    for i in range(32):
+        u0, u1 = s_ref[b, start + i], s_ref[b, start + 32 + i]
+        v0, v1 = s_ref[b, start + 127 - i], s_ref[b, start + 95 - i]
+        h0, h1 = jnp.maximum(u0, v0), jnp.maximum(u1, v1)
+        l0, l1 = jnp.minimum(u0, v0), jnp.minimum(u1, v1)
+        x_ref[b, i] = jnp.maximum(h0, h1)
+        x_ref[b, 32 + i] = jnp.minimum(h0, h1)
+        x_ref[b, 64 + i] = jnp.maximum(l0, l1)
+        x_ref[b, 96 + i] = jnp.minimum(l0, l1)
+
+    @pl.loop(0, 4, unroll=2)
+    def _(k):
+        x = clean([x_ref[b, k * 32 + i] for i in range(32)])
         for i in range(32):
-            u0, u1 = s_ref[b, base + i], s_ref[b, base + 32 + i]
-            v0, v1 = s_ref[b, base + 127 - i], s_ref[b, base + 95 - i]
-            h0, h1 = jnp.maximum(u0, v0), jnp.maximum(u1, v1)
-            l0, l1 = jnp.minimum(u0, v0), jnp.minimum(u1, v1)
-            x_ref[dst, i] = jnp.maximum(h0, h1)
-            x_ref[dst, 32 + i] = jnp.minimum(h0, h1)
-            x_ref[dst, 64 + i] = jnp.maximum(l0, l1)
-            x_ref[dst, 96 + i] = jnp.minimum(l0, l1)
-
-        @pl.loop(0, 4, unroll=2)
-        def _(k):
-            x = clean([x_ref[dst, k * 32 + i] for i in range(32)])
-            for i in range(32):
-                s_ref[b, base + k * 32 + i] = x[i]
-
+            s_ref[b, start + k * 32 + i] = x[i]
+
+
+def join_halves(s_ref, x_ref, b):
     for i in range(32):
         t = clean([jnp.maximum(s_ref[b, i + 32 * k], s_ref[b, 255 - i - 32 * k]) for k in range(4)])
         for k in range(4):
-            x_ref[dst, i + 32 * k] = t[k]
+            x_ref[b, i + 32 * k] = t[k]
 
     @pl.loop(0, 4, unroll=2)
     def _(k):
-        x = clean([x_ref[dst, k * 32 + i] for i in range(32)])
+        x = clean([x_ref[b, k * 32 + i] for i in range(32)])
         for i in range(32):
-            x_ref[dst, k * 32 + i] = x[i]
+            x_ref[b, k * 32 + i] = x[i]
 
 
 def merge_pair(x_ref, y_ref, b0, b1, dst, level):
@@ -194,7 +194,7 @@
 def kernel(
     n_cap, sizes_in, q_in, probes_in, book_in, codes_ref, out_ref,
     sizes_ref, q_ref, probes_ref, book_ref, send_ref, rows_ref, own_ref, t_ref, d_own, d_peer, table_ref,
-    s_ref, x_ref, y_ref, z_ref, best_ref, back_ref, idx_ref,
+    mine_ref, s_ref, x_ref, y_ref, z_ref, best_ref, back_ref, idx_ref,
     small_sem, in_sem, code_send, code_recv, row_send, row_recv, best_send, best_recv, row_keep, best_keep,
 ):
     chunks, n_dev, chip_slots, width = send_ref.shape
@@ -290,25 +290,33 @@
             for p in range(each, part_dev):
                 swaps[p].start()
         rows = rows_ref[c].reshape(n_dev * chip_slots, width)
+        n_half = half // SUBL
         for e in range(each):
-            p = c * each + e
             m = lax.broadcasted_iota(jnp.int32, (256, rows.shape[0]), 0)
             want = ((m // 128) * 32 + m % 32) * chip_slots + e * n_cap + (m % 128) // 32
             pick = jnp.where(lax.broadcasted_iota(jnp.int32, m.shape, 1) == want, 1.0, 0.0).astype(jnp.bfloat16)
-            mine = jnp.dot(pick, rows, preferred_element_type=jnp.float32).astype(jnp.bfloat16)
-            for which, ref in enumerate((d_own, d_peer)):
+            mine_ref[e] = jnp.dot(pick, rows, preferred_element_type=jnp.float32).astype(jnp.bfloat16)
+        for which, ref in enumerate((d_own, d_peer)):
+            first = half * (rep if which == 0 else 1 - rep)
+            for e in range(each):
+                p = c * each + e
                 if which == 1:
                     swaps[p].wait_recv()
-                sc = lax.dot_general(ref[p], mine, (((1,), (1,)), ((), ())), preferred_element_type=jnp.float32)
-                first = half * (rep if which == 0 else 1 - rep)
+                sc = lax.dot_general(
+                    ref[p], mine_ref[e], (((1,), (1,)), ((), ())), preferred_element_type=jnp.float32
+                )
                 ok = lax.broadcasted_iota(jnp.int32, (half, LANES), 0) + first < sizes_ref[p]
                 for h in range(2):
                     blk = jnp.where(ok, sc[:, h * LANES : (h + 1) * LANES], MASKED)
-                    s_ref[h, pl.ds(which * half // SUBL, half // SUBL)] = blk.reshape(half // SUBL, SUBL, LANES)
-
-            @pl.loop(0, 2)
-            def _(h):
-                sort_block(s_ref, x_ref, h, e * 2 + h)
+                    s_ref[e * 2 + h, pl.ds(which * n_half, n_half)] = blk.reshape(n_half, SUBL, LANES)
+
+            @pl.loop(0, 2 * each)
+            def _(b):
+                sort_half(s_ref, x_ref, b, which * n_half)
+
+        @pl.loop(0, 2 * each)
+        def _(b):
+            join_halves(s_ref, x_ref, b)
 
         @pl.loop(0, 2)
         def _(b):
@@ -419,7 +427,8 @@
             decoded,
             decoded,
             vmem((book.shape[1], groups, LANES), jnp.float32),
-            vmem((2, 2 * half // SUBL, SUBL, LANES), jnp.float32),
+            vmem((2, 256, width), jnp.bfloat16),
+            vmem((4, 2 * half // SUBL, SUBL, LANES), jnp.float32),
             vmem((4, RANKS, SUBL, LANES), jnp.float32),
             vmem((RANKS, SUBL, LANES), jnp.float32),
             vmem((RANKS * SUBL, LANES), jnp.float32),

time: 50.9 us -> 49 us (0.963)
  Pallas kernels: 50.2 us -> 48.3 us
    pallas_call x1, Pallas kernels: 50.2 us -> 48.3 us  [local(): pl.pallas_call(functools.partial(kernel, n_cap), out_shape=jax.ShapeDtype...]
where the time goes in v9:
time: 49 us; the launch traced here: 48.9 us
  Pallas kernels  48.3 us (99%)
  local copies, waits for them, and re-layouts  0.62 us (1%)
    pallas_call x1, Pallas kernels, local(): pl.pallas_call(functools.partial(kernel, n_cap), out_shape=jax.ShapeDtype...  48.3 us

profile of v9, /device:TPU:0, one launch (start us, length us, event | category | flops | bytes accessed | tf_op | source)
XLA Modules:
  0.0 48.9 jit_solution(13108168399688754414)
XLA Ops:
  0.0 48.3 %search.1 = f32[64,100]{1,0:T(8,128)S(1)} custom-call(s32[4]{0:T(128)} %sizes_in.1, bf16[64,768]{1,0:T(8,128)(2,1)} %q_in.1, s32[8,64]{1,0:T(8,128)} %bitcast.3, bf16[16,4,192]{2,1,0:T(4,128)(2,1)} %bitcast.2, s32[4,192,1024]{2,1,0:T(8,128)} %codes_ref.1), custom_call_target="tpu_custom_call" | custom-call | tf_op jit(solution)/shard_map/search/pallas_call | solution.py:413
  48.3 0.6 %copy.7 = f32[64,100]{1,0:T(8,128)} copy(f32[64,100]{1,0:T(8,128)S(1)} %search.1) | data formatting | bytes 51200

commit v10 on v9

--- a/solution.py
+++ b/solution.py
@@ -194,7 +194,7 @@
 def kernel(
     n_cap, sizes_in, q_in, probes_in, book_in, codes_ref, out_ref,
     sizes_ref, q_ref, probes_ref, book_ref, send_ref, rows_ref, own_ref, t_ref, d_own, d_peer, table_ref,
-    mine_ref, s_ref, x_ref, y_ref, z_ref, best_ref, back_ref, idx_ref,
+    pick_ref, choice_ref, mine_ref, s_ref, x_ref, y_ref, z_ref, best_ref, back_ref, idx_ref,
     small_sem, in_sem, code_send, code_recv, row_send, row_recv, best_send, best_recv, row_keep, best_keep,
 ):
     chunks, n_dev, chip_slots, width = send_ref.shape
@@ -283,6 +283,12 @@
         if p < each:
             swaps[p].start()
     send_rows(1)
+    for e in range(each):
+        m = lax.broadcasted_iota(jnp.int32, pick_ref.shape[1:], 0)
+        want = ((m // 128) * 32 + m % 32) * chip_slots + e * n_cap + (m % 128) // 32
+        here = lax.broadcasted_iota(jnp.int32, m.shape, 1)
+        pick_ref[e] = jnp.where(here == want, 1.0, 0.0).astype(jnp.bfloat16)
+    fill_choice(idx_ref, choice_ref)
 
     for c in range(chunks):
         finish_recv(send_ref.at[c], rows_ref.at[c], row_recv.at[c], row_keep.at[c])
@@ -292,10 +298,7 @@
         rows = rows_ref[c].reshape(n_dev * chip_slots, width)
         n_half = half // SUBL
         for e in range(each):
-            m = lax.broadcasted_iota(jnp.int32, (256, rows.shape[0]), 0)
-            want = ((m // 128) * 32 + m % 32) * chip_slots + e * n_cap + (m % 128) // 32
-            pick = jnp.where(lax.broadcasted_iota(jnp.int32, m.shape, 1) == want, 1.0, 0.0).astype(jnp.bfloat16)
-            mine_ref[e] = jnp.dot(pick, rows, preferred_element_type=jnp.float32).astype(jnp.bfloat16)
+            mine_ref[e] = jnp.dot(pick_ref[e], rows, preferred_element_type=jnp.float32).astype(jnp.bfloat16)
         for which, ref in enumerate((d_own, d_peer)):
             first = half * (rep if which == 0 else 1 - rep)
             for e in range(each):
@@ -336,7 +339,7 @@
     found = None
     for c in range(chunks):
         finish_recv(best_ref.at[c], back_ref.at[c], best_recv.at[c], best_keep.at[c])
-        got = select_lists(idx_ref, back_ref[c].reshape(n_dev * chip_slots, RANKS), c)
+        got = select_lists(choice_ref[c], back_ref[c].reshape(n_dev * chip_slots, RANKS))
         found = got if found is None else found + got
     final_merge(found, out_ref)
     for c in range(chunks):
@@ -346,18 +349,22 @@
         c.wait_send()
 
 
-def select_lists(idx_ref, lists, c):
-    n_slots = lists.shape[0]
+def fill_choice(idx_ref, choice_ref):
+    chunks, n_slots, n_lists = choice_ref.shape
     wanted = jnp.concatenate([idx_ref[k : k + 1, :] for k in range(idx_ref.shape[0])], axis=1)
-    slot = lax.broadcasted_iota(jnp.int32, (n_slots, wanted.shape[1]), 0) + c * n_slots
-    pick = jnp.where(slot == wanted, 1.0, 0.0).astype(jnp.bfloat16)
+    slot = lax.broadcasted_iota(jnp.int32, (n_slots, n_lists), 0)
+    for c in range(chunks):
+        choice_ref[c] = jnp.where(slot == wanted - c * n_slots, 1.0, 0.0).astype(jnp.bfloat16)
+
+
+def select_lists(choice, lists):
     rest = lists.T
     parts = []
     for _ in range(3):
         part = rest.astype(jnp.bfloat16)
         rest = rest - part.astype(jnp.float32)
         parts.append(part)
-    got = jnp.dot(jnp.concatenate(parts, axis=0), pick, preferred_element_type=jnp.float32)
+    got = jnp.dot(jnp.concatenate(parts, axis=0), choice, preferred_element_type=jnp.float32)
     return got[:RANKS] + got[RANKS : 2 * RANKS] + got[2 * RANKS :]
 
 
@@ -427,6 +434,8 @@
             decoded,
             decoded,
             vmem((book.shape[1], groups, LANES), jnp.float32),
+            vmem((part_dev // chunks, 256, n_dev * chip_slots), jnp.bfloat16),
+            vmem((chunks, n_dev * chip_slots, n_probe * own_rows), jnp.bfloat16),
             vmem((2, 256, width), jnp.bfloat16),
             vmem((4, 2 * half // SUBL, SUBL, LANES), jnp.float32),
             vmem((4, RANKS, SUBL, LANES), jnp.float32),

time: 49 us -> 49 us (level)
  no operation moved by 1% of the time
where the time goes in v10:
time: 49 us; the launch traced here: 48.9 us
  Pallas kernels  48.2 us (98%)
  local copies, waits for them, and re-layouts  0.62 us (1%)
    pallas_call x1, Pallas kernels, local(): pl.pallas_call(functools.partial(kernel, n_cap), out_shape=jax.ShapeDtype...  48.2 us

profile of v10, /device:TPU:0, one launch (start us, length us, event | category | flops | bytes accessed | tf_op | source)
XLA Modules:
  0.0 48.9 jit_solution(4781115460211528986)
XLA Ops:
  0.0 48.2 %search.1 = f32[64,100]{1,0:T(8,128)S(1)} custom-call(s32[4]{0:T(128)} %sizes_in.1, bf16[64,768]{1,0:T(8,128)(2,1)} %q_in.1, s32[8,64]{1,0:T(8,128)} %bitcast.3, bf16[16,4,192]{2,1,0:T(4,128)(2,1)} %bitcast.2, s32[4,192,1024]{2,1,0:T(8,128)} %codes_ref.1), custom_call_target="tpu_custom_call" | custom-call | tf_op jit(solution)/shard_map/search/pallas_call | solution.py:420
  48.2 0.6 %copy.7 = f32[64,100]{1,0:T(8,128)} copy(f32[64,100]{1,0:T(8,128)S(1)} %search.1) | data formatting | bytes 51200
